TPU v7x, 32 devices: a whole 2x2x4 slice. The times are simulated.
32 devices in a mesh: seq: 4 (over x, core), fsdp: 8 (over z, y).
Axes of the slice: x: 2, y: 2, z: 4, core: 2. Of those that a mesh axis runs over, the one named last changes fastest.
Arguments:
- tokens: bfloat16 [2048, 8, 768], P(('seq', 'fsdp')), may hold values from -6 to 6
- pass_index: int32 [2048, 8], P(('seq', 'fsdp')), may hold values from 0 to 4
- lengths: int32 [8], replicated, may hold values from 1 to 2048, 12288 in all
- table: bfloat16 [5, 768], replicated, may hold values from -3 to 3
- gain_attn: bfloat16 [768], P('fsdp'), may hold values from 0.5 to 1.5
- w_qkv: bfloat16 [768, 2304], P('fsdp'), may hold values from -0.21875 to 0.21875
- w_out: bfloat16 [768, 768], P('fsdp'), may hold values from -1.25 to 1.25
- gain_mlp: bfloat16 [768], P('fsdp'), may hold values from 0.5 to 1.5
- w_up: bfloat16 [768, 3072], P('fsdp'), may hold values from -0.21875 to 0.21875
- w_down: bfloat16 [3072, 768], P('fsdp'), may hold values from -0.109375 to 0.109375
- cotangent: bfloat16 [2048, 8, 768], P(('seq', 'fsdp')), may hold values from -6 to 6
Outputs:
- output: bfloat16 [2048, 8, 768], P(('seq', 'fsdp'))
- d_tokens: bfloat16 [2048, 8, 768], P(('seq', 'fsdp'))
- d_table: float32 [5, 768], replicated
- d_gain_attn: float32 [768], P('fsdp')
- d_w_qkv: float32 [768, 2304], P('fsdp')
- d_w_out: float32 [768, 768], P('fsdp')
- d_gain_mlp: float32 [768], P('fsdp')
- d_w_up: float32 [768, 3072], P('fsdp')
- d_w_down: float32 [3072, 768], P('fsdp')
Inputs may be any that keep to these rules, and one draw needn't show every extreme that they name: The longest sequence is exactly 2048 long; all lengths add up to 12288.
All inputs are finite; a program needn't handle non-finite values.
Results may differ from a plain program's by a relative error of at most 0.013.
Values may be sent and summed in bfloat16 or wider, within the bound.
No kernel may reach another device: no remote copies, remote signals or barrier semaphores. Data moves between devices by JAX's collectives and lax.ppermute only.
A program may use at most 192 MiB of HBM per device.

v0:
```python
import jax
import jax.numpy as jnp
from jax import lax
from jax.sharding import PartitionSpec as P

HEADS = 12


EPSILON = 1e-05
MASKED = -1e30


def as_sent(value):
    return jax.tree.map(lambda a: a.astype(jnp.bfloat16) if a.dtype == jnp.float32 else a, value)


def norm_rows(values, gain_vec):
    centre = jnp.mean(values, axis=-1, keepdims=True)
    shifted = values - centre
    spread = jnp.mean(shifted * shifted, axis=-1, keepdims=True)
    return shifted * lax.rsqrt(spread + EPSILON) * gain_vec


def gelu_tanh(values):
    return jax.nn.gelu(values, approximate=True)


def visible(first_row, row_count, reach_to, length):
    query_at = first_row + jnp.arange(row_count, dtype=jnp.int32)[:, None]
    key_at = jnp.arange(reach_to, dtype=jnp.int32)[None, :]
    return (query_at >= key_at) & (key_at < length)


def block_scores(queries, keys_all, first_row, row_count, length):
    reach_to = first_row + row_count
    scaling = queries.shape[-1] ** (-0.5)
    scores = (
        jnp.einsum(
            "qhd,khd->hqk",
            queries[first_row:reach_to],
            keys_all[:reach_to],
            preferred_element_type=jnp.float32,
        )
        * scaling
    )
    return jnp.where(visible(first_row, row_count, reach_to, length)[None], scores, MASKED)


def attend(packed, length):
    queries, keys_all, values_all = (packed[:, 0], packed[:, 1], packed[:, 2])
    span_len = packed.shape[0]
    block_len = min(512, span_len)
    outputs = []
    totals = []
    for first_row in range(0, span_len, block_len):
        scores = block_scores(queries, keys_all, first_row, block_len, length)
        highest = jnp.max(scores, axis=-1, keepdims=True)
        log_total = highest + jnp.log(jnp.sum(jnp.exp(scores - highest), axis=-1, keepdims=True))
        weights = jnp.exp(scores - log_total).astype(jnp.bfloat16)
        mixed = jnp.einsum(
            "hqk,khd->qhd",
            weights,
            values_all[: first_row + block_len],
            preferred_element_type=jnp.float32,
        )
        outputs.append(mixed.astype(jnp.bfloat16))
        totals.append(log_total[..., 0])
    return (jnp.concatenate(outputs, axis=0), jnp.concatenate(totals, axis=1))


def attend_back(packed, d_out, totals, length):
    queries, keys_all, values_all = (packed[:, 0], packed[:, 1], packed[:, 2])
    span_len, heads_here, head_size = queries.shape
    block_len = min(512, span_len)
    scaling = head_size ** (-0.5)
    d_queries = []
    d_keys = jnp.zeros((span_len, heads_here, head_size), jnp.float32)
    d_values = jnp.zeros((span_len, heads_here, head_size), jnp.float32)
    for first_row in range(0, span_len, block_len):
        reach_to = first_row + block_len
        scores = block_scores(queries, keys_all, first_row, block_len, length)
        probs = jnp.exp(scores - totals[:, first_row:reach_to, None])
        weights = probs.astype(jnp.bfloat16)
        d_block = d_out[first_row:reach_to]
        d_probs = jnp.einsum(
            "qhd,khd->hqk", d_block, values_all[:reach_to], preferred_element_type=jnp.float32
        )
        inner_sum = jnp.sum(probs * d_probs, axis=-1, keepdims=True)
        d_scores = (probs * (d_probs - inner_sum)).astype(jnp.bfloat16)
        d_queries.append(
            jnp.einsum(
                "hqk,khd->qhd", d_scores, keys_all[:reach_to], preferred_element_type=jnp.float32
            )
            * scaling
        )
        d_keys = d_keys.at[:reach_to].add(
            jnp.einsum(
                "hqk,qhd->khd",
                d_scores,
                queries[first_row:reach_to],
                preferred_element_type=jnp.float32,
            )
            * scaling
        )
        d_values = d_values.at[:reach_to].add(
            jnp.einsum("hqk,qhd->khd", weights, d_block, preferred_element_type=jnp.float32)
        )
    d_query_all = jnp.concatenate(d_queries, axis=0).astype(jnp.bfloat16)
    return jnp.stack(
        (d_query_all, d_keys.astype(jnp.bfloat16), d_values.astype(jnp.bfloat16)), axis=1
    )


def per_device(
    tokens, pass_index, lengths, table, gain_attn, w_qkv, w_out, gain_mlp, w_up, w_down, cotangent
):
    group_count = lax.axis_size("fsdp")
    seq_count = lax.axis_size("seq")
    local_len, seq_total, model_width = tokens.shape
    per_group = seq_total // group_count
    heads_here = HEADS // seq_count
    head_size = model_width // HEADS
    part_width = model_width // seq_count
    chooser = (pass_index[..., None] == jnp.arange(table.shape[0], dtype=jnp.int32)).astype(
        jnp.bfloat16
    )
    embedded = jnp.einsum("pnc,cd->pnd", chooser, table, preferred_element_type=jnp.float32)
    summed_in = (tokens.astype(jnp.float32) + embedded).astype(jnp.bfloat16)
    dealt_shape = (local_len, group_count, per_group, model_width)
    arrived, cot_arrived = (
        lax.all_to_all(
            summed_in.reshape(dealt_shape), "fsdp", split_axis=1, concat_axis=0, tiled=True
        ),
        lax.all_to_all(
            cotangent.reshape(dealt_shape), "fsdp", split_axis=1, concat_axis=0, tiled=True
        ),
    )
    span_len = arrived.shape[0]
    row_total = span_len * per_group
    inputs_b = arrived.reshape(row_total, model_width)
    cot_rows = cot_arrived.reshape(row_total, model_width)
    my_lengths = lax.dynamic_slice_in_dim(lengths, lax.axis_index("fsdp") * per_group, per_group)
    shard_set = (gain_attn, w_qkv, w_out, gain_mlp, w_up, w_down)
    gathered = (
        lax.all_gather(shard_set[0], "fsdp", axis=0, tiled=True),
        lax.all_gather(shard_set[1], "fsdp", axis=0, tiled=True),
        lax.all_gather(shard_set[2], "fsdp", axis=0, tiled=True),
        lax.all_gather(shard_set[3], "fsdp", axis=0, tiled=True),
        lax.all_gather(shard_set[4], "fsdp", axis=0, tiled=True),
        lax.all_gather(shard_set[5], "fsdp", axis=0, tiled=True),
    )
    gain_one = gathered[0].astype(jnp.float32)
    gain_two = gathered[3].astype(jnp.float32)
    inputs_f = inputs_b.astype(jnp.float32)
    normed = norm_rows(inputs_f, gain_one).astype(jnp.bfloat16)
    projected = jnp.dot(normed, gathered[1], preferred_element_type=jnp.float32).astype(
        jnp.bfloat16
    )
    head_parts = lax.all_to_all(
        projected.reshape(span_len, per_group, 3, seq_count, part_width),
        "seq",
        split_axis=3,
        concat_axis=0,
        tiled=True,
    )
    seq_len = head_parts.shape[0]
    packed_all = jnp.moveaxis(
        head_parts.reshape(seq_len, per_group, 3, heads_here, head_size), 1, 0
    )
    attended, log_totals = lax.map(
        lambda bundle: attend(bundle[0], bundle[1]), (packed_all, my_lengths)
    )
    back_heads = jnp.moveaxis(attended, 0, 1).reshape(seq_len, per_group, 1, part_width)
    attended_rows = (
        lax.all_to_all(as_sent(back_heads), "seq", split_axis=0, concat_axis=2, tiled=True)
        .astype(back_heads.dtype)
        .reshape(row_total, model_width)
    )
    residual = inputs_f + jnp.dot(attended_rows, gathered[2], preferred_element_type=jnp.float32)
    normed_mlp = norm_rows(residual, gain_two).astype(jnp.bfloat16)
    upper = jnp.dot(normed_mlp, gathered[4], preferred_element_type=jnp.float32)
    activation = gelu_tanh(upper).astype(jnp.bfloat16)
    result = (
        residual + jnp.dot(activation, gathered[5], preferred_element_type=jnp.float32)
    ).astype(jnp.bfloat16)
    return_shape = (span_len, 1, per_group, model_width)
    out_back = lax.all_to_all(
        result.reshape(return_shape), "fsdp", split_axis=0, concat_axis=1, tiled=True
    )
    gathered = (
        lax.all_gather(shard_set[0], "fsdp", axis=0, tiled=True),
        lax.all_gather(shard_set[1], "fsdp", axis=0, tiled=True),
        lax.all_gather(shard_set[2], "fsdp", axis=0, tiled=True),
        lax.all_gather(shard_set[3], "fsdp", axis=0, tiled=True),
        lax.all_gather(shard_set[4], "fsdp", axis=0, tiled=True),
        lax.all_gather(shard_set[5], "fsdp", axis=0, tiled=True),
    )
    grad_down = jnp.einsum("rf,rd->fd", activation, cot_rows, preferred_element_type=jnp.float32)
    d_act = jnp.einsum("rd,fd->rf", cot_rows, gathered[5], preferred_element_type=jnp.float32)
    d_upper = jax.vjp(gelu_tanh, upper)[1](d_act)[0].astype(jnp.bfloat16)
    grad_up = jnp.einsum("rd,rf->df", normed_mlp, d_upper, preferred_element_type=jnp.float32)
    d_normed_mlp = jnp.einsum("rf,df->rd", d_upper, gathered[4], preferred_element_type=jnp.float32)
    d_res_norm, grad_gain_mlp = jax.vjp(norm_rows, residual, gain_two)[1](d_normed_mlp)
    d_residual = cot_rows.astype(jnp.float32) + d_res_norm
    d_branch = d_residual.astype(jnp.bfloat16)
    grad_out = jnp.einsum("re,rd->ed", attended_rows, d_branch, preferred_element_type=jnp.float32)
    d_attended = jnp.einsum(
        "rd,ed->re", d_branch, gathered[2], preferred_element_type=jnp.float32
    ).astype(jnp.bfloat16)
    d_heads = lax.all_to_all(
        d_attended.reshape(span_len, per_group, seq_count, part_width),
        "seq",
        split_axis=2,
        concat_axis=0,
        tiled=True,
    )
    d_items = jnp.moveaxis(d_heads.reshape(seq_len, per_group, heads_here, head_size), 1, 0)
    d_packed = lax.map(
        lambda bundle: attend_back(bundle[0], bundle[1], bundle[2], bundle[3]),
        (packed_all, d_items, log_totals, my_lengths),
    )
    d_parts = jnp.moveaxis(d_packed, 0, 1).reshape(seq_len, per_group, 3, 1, part_width)
    d_projected = (
        lax.all_to_all(as_sent(d_parts), "seq", split_axis=0, concat_axis=3, tiled=True)
        .astype(d_parts.dtype)
        .reshape(row_total, 3 * model_width)
    )
    grad_qkv = jnp.einsum("rd,rc->dc", normed, d_projected, preferred_element_type=jnp.float32)
    d_normed = jnp.einsum("rc,dc->rd", d_projected, gathered[1], preferred_element_type=jnp.float32)
    d_in_norm, grad_gain_attn = jax.vjp(norm_rows, inputs_f, gain_one)[1](d_normed)
    d_inputs = (d_residual + d_in_norm).astype(jnp.bfloat16)
    d_back = lax.all_to_all(
        d_inputs.reshape(return_shape), "fsdp", split_axis=0, concat_axis=1, tiled=True
    )
    output = out_back.reshape(local_len, seq_total, model_width)
    d_tokens = d_back.reshape(local_len, seq_total, model_width)
    grad_table = jnp.einsum("pnc,pnd->cd", chooser, d_tokens, preferred_element_type=jnp.float32)
    grad_table = lax.psum(grad_table, ("seq", "fsdp"))
    owned = (
        lax.psum_scatter(grad_gain_attn, "fsdp", scatter_dimension=0, tiled=True),
        lax.psum_scatter(grad_qkv, "fsdp", scatter_dimension=0, tiled=True),
        lax.psum_scatter(grad_out, "fsdp", scatter_dimension=0, tiled=True),
        lax.psum_scatter(grad_gain_mlp, "fsdp", scatter_dimension=0, tiled=True),
        lax.psum_scatter(grad_up, "fsdp", scatter_dimension=0, tiled=True),
        lax.psum_scatter(grad_down, "fsdp", scatter_dimension=0, tiled=True),
    )
    owned = (
        lax.psum(owned[0].astype(jnp.bfloat16), "seq").astype(jnp.float32),
        lax.psum(owned[1].astype(jnp.bfloat16), "seq").astype(jnp.float32),
        lax.psum(owned[2].astype(jnp.bfloat16), "seq").astype(jnp.float32),
        lax.psum(owned[3].astype(jnp.bfloat16), "seq").astype(jnp.float32),
        lax.psum(owned[4].astype(jnp.bfloat16), "seq").astype(jnp.float32),
        lax.psum(owned[5].astype(jnp.bfloat16), "seq").astype(jnp.float32),
    )
    return (
        output,
        d_tokens,
        grad_table,
        owned[0],
        owned[1],
        owned[2],
        owned[3],
        owned[4],
        owned[5],
    )


def solution(mesh):
    return jax.shard_map(
        per_device,
        mesh=mesh,
        in_specs=(
            P(("seq", "fsdp"), None, None),
            P(("seq", "fsdp"), None),
            P(),
            P(),
            P("fsdp"),
            P("fsdp", None),
            P("fsdp", None),
            P("fsdp"),
            P("fsdp", None),
            P("fsdp", None),
            P(("seq", "fsdp"), None, None),
        ),
        out_specs=(
            P(("seq", "fsdp"), None, None),
            P(("seq", "fsdp"), None, None),
            P(),
            P("fsdp"),
            P("fsdp", None),
            P("fsdp", None),
            P("fsdp"),
            P("fsdp", None),
            P("fsdp", None),
        ),
        check_vma=False,
    )
```

profile of v0, /device:TPU:0, one launch (start us, length us, event | category | flops | bytes accessed | tf_op | source)
XLA Modules:
  0.0 1099.9 jit_solution(12818097148169739574)
XLA Ops:
  12.9 7.3 all-to-all-start
  22.5 38.0 %all-reduce.7 = (bf16[768]{0:T(1024)(128)(2,1)S(1)}, bf16[768]{0:T(1024)(128)(2,1)S(1)}) all-reduce(bf16[768]{0:T(1024)(128)(2,1)S(1)} %dynamic-update-slice.28, bf16[768]{0:T(1024)(128)(2,1)S(1)} %dynamic-update-slice.29), channel_id=1, replica_groups=mesh['seq'=4,'fsdp'=8] {'fsdp'}, use_global_device_ids=true, to_apply=%add.2 | all-reduce | flops 1536 | bytes 6144
  65.9 26.0 %all-gather.5.cloned.1.call-done = bf16[768,2304]{1,0:T(8,128)(2,1)} async-done(((bf16[96,2304]{1,0:T(8,128)(2,1)}), bf16[768,2304]{1,0:T(8,128)(2,1)}) %all-gather.5.cloned.1.call-update) | async-done | bytes 3538960 | tf_op jit(solution)/shard_map/all_gather | solution.py:146
  91.8 5.4 convolution_convert_fusion
  97.2 2.9 copy.177
  101.8 4.6 all-to-all-start.1
  110.1 24.9 %all-to-all-done.1 = bf16[512,1,3,4,192]{0,4,2,1,3:T(8,128)(2,1)} async-done(((bf16[512,1,3,4,192]{0,4,2,1,3:T(8,128)(2,1)}), bf16[512,1,3,4,192]{0,4,2,1,3:T(8,128)(2,1)}, u32[]{:S(2)}, u32[]{:S(2)}) %all-to-all-start.1) | async-done | bytes 2359328 | tf_op jit(solution)/shard_map/all_to_all | solution.py:159
  135.0 4.7 all-to-all-start.4
  139.7 4.9 copy.179
  144.7 5.9 squeeze.44
  158.5 3.0 exponential_reduce_fusion.1
  164.4 5.9 fusion
  172.8 6.8 exponential_reduce_fusion
  179.6 6.4 fusion.56
  192.4 3.7 all-to-all-start.2
  196.1 7.9 fusion.89
  204.0 3.6 all-to-all-done.2
  207.7 2.6 reshape.803
  210.3 5.7 copy.182
  219.4 9.7 all-gather.7.cloned.1.call-done
  233.0 76.2 %all-gather.9.cloned.1.call-done = bf16[768,3072]{1,0:T(8,128)(2,1)} async-done(((bf16[96,3072]{1,0:T(8,128)(2,1)}), bf16[768,3072]{1,0:T(8,128)(2,1)}) %all-gather.9.cloned.1.call-update) | async-done | bytes 4718608 | tf_op jit(solution)/shard_map/all_gather | solution.py:149
  309.2 12.9 %fusion.9 = (bf16[512,3072]{1,0:T(8,128)(2,1)S(1)}, f32[512,3072]{1,0:T(8,128)}) fusion(f32[512,3072]{1,0:T(8,128)} %fusion.89, bf16[768,3072]{1,0:T(8,128)(2,1)} %all-gather.9.cloned.1.call-done, f32[512,768]{1,0:T(8,128)} %copy-done.20, f32[768]{0:T(1024)S(1)} %convert_element_type.211, f32[512]{0:T(512)S(1)} %fusion.71, f32[512]{0:T(512)S(1)} %broadcast_multiply_fusion.1), kind=kOutput, calls=%fused_computation.21 | convolution fusion | flops 2448949248 | bytes 22027264 | tf_op jit(solution)/shard_map/dot_general | solution.py:181
  322.1 2.9 multiply_reduce_fusion.4
  332.2 4.2 all-to-all-start.5
  339.1 9.0 all-to-all-done.5
  350.2 3.0 convolution_bitcast_fusion.3
  353.2 2.9 multiply_reduce_fusion.3
  356.2 4.6 multiply_reduce_fusion.2
  364.1 6.4 multiply_reduce_fusion.1
  370.5 3.8 fusion.19
  374.4 8.6 multiply_reduce_fusion
  383.0 5.8 fusion.23
  388.8 5.9 copy.193
  394.7 3.1 multiply_convert_fusion.4
  399.9 3.9 multiply_convert_fusion.2
  403.8 3.5 fusion.49
  408.7 9.0 multiply_convert_fusion.1
  417.7 5.6 fusion.17
  423.4 3.9 multiply_convert_fusion
  430.0 3.9 copy.192
  436.0 3.2 fusion.53
  441.8 3.2 fusion.54
  445.1 3.8 copy.191
  448.9 10.4 pad_maximum_fusion
  459.3 5.0 all-to-all-start.6
  465.6 46.9 %all-to-all-done.6 = bf16[2048,1,3,1,192]{4,2,3,1,0:T(4,128)(2,1)} async-done(((bf16[2048,1,3,1,192]{4,2,3,1,0:T(4,128)(2,1)}), bf16[2048,1,3,1,192]{4,2,3,1,0:T(4,128)(2,1)}, u32[]{:S(2)}, u32[]{:S(2)}) %all-to-all-start.6) | async-done | bytes 2359328 | tf_op jit(solution)/shard_map/all_to_all | solution.py:224
  512.5 7.2 copy.203
  521.7 5.0 fusion.90
  528.0 7.2 fusion.82
  535.7 9.8 fusion.84
  545.5 8.9 fusion.44
  554.4 3.2 reduce.25
  557.6 3.0 reshape.804
  560.6 4.4 all-to-all-start.3
  565.0 4.3 fusion.42
  574.9 31.0 %all-to-all-done.3 = bf16[8,2,24576]{2,1,0:T(2,128)(2,1)} async-done(((bf16[8,2,24576]{2,1,0:T(2,128)(2,1)}), bf16[8,2,24576]{2,1,0:T(2,128)(2,1)}, u32[]{:S(2)}, u32[]{:S(2)}) %all-to-all-start.3) | async-done | bytes 786464 | tf_op jit(solution)/shard_map/all_to_all | solution.py:187
  605.8 3.5 all-to-all-start.7
  611.1 70.3 %reduce-scatter.5.cloned.1.call-done = f32[96,2304]{1,0:T(8,128)} async-done(((f32[768,2304]{1,0:T(8,128)}), f32[96,2304]{1,0:T(8,128)}) %reduce-scatter.5.cloned.1.call-update) | async-done | bytes 884752 | tf_op jit(solution)/shard_map/reduce_scatter | solution.py:241
  683.5 162.8 %reduce-scatter.9.cloned.1.call-done = f32[96,3072]{1,0:T(8,128)} async-done(((f32[768,3072]{1,0:T(8,128)}), f32[96,3072]{1,0:T(8,128)}) %reduce-scatter.9.cloned.1.call-update) | async-done | bytes 1179664 | tf_op jit(solution)/shard_map/reduce_scatter | solution.py:244
  848.5 162.7 %reduce-scatter.11.cloned.1.call-done = f32[384,768]{1,0:T(8,128)} async-done(((f32[3072,768]{1,0:T(8,128)}), f32[384,768]{1,0:T(8,128)}) %reduce-scatter.11.cloned.1.call-update) | async-done | bytes 1179664 | tf_op jit(solution)/shard_map/reduce_scatter | solution.py:245
  1014.0 4.1 reshape.805
  1019.5 19.7 %all-reduce.6 = (bf16[768]{0:T(1024)(128)(2,1)S(1)}, bf16[768]{0:T(1024)(128)(2,1)S(1)}) all-reduce(f32[768]{0:T(1024)S(1)} %get-tuple-element.259, f32[768]{0:T(1024)S(1)} %get-tuple-element.257), channel_id=2, replica_groups=mesh['seq'=4,'fsdp'=8] {'fsdp'}, use_global_device_ids=true, to_apply=%region_22.23.clone | all-reduce | flops 1536 | bytes 9216
  1039.4 5.6 all-reduce.8
  1048.6 37.7 %psum.49 = f32[5,768]{1,0:T(8,128)} all-reduce(f32[5,768]{1,0:T(8,128)S(1)} %convolution_bitcast_fusion.4), channel_id=1, replica_groups=mesh['seq'=4,'fsdp'=8] {'seq','fsdp'}, use_global_device_ids=true, to_apply=%region_20.21 | all-reduce | flops 3840 | bytes 30720 | tf_op jit(solution)/shard_map/psum | solution.py:238
  (292 shorter events, 101.3 us)
Async XLA Ops:
  7.2 84.6 %all-gather.5.cloned.1.call-start = ((), (), s32[]{:S(2)}) async-start(), calls=%async_computation.12 | async-start | bytes 3981312 | tf_op jit(solution)/shard_map/all_gather | solution.py:146
  7.9 12.8 %copy-start.54 = (u32[32]{0:T(128)S(1)}, u32[32]{0:T(128)}, u32[]{:S(2)}) copy-start(u32[32]{0:T(128)} %constant.337) | copy-start | bytes 388
  7.9 14.1 %copy-start.57 = (bf16[96]{0:T(256)(128)(2,1)S(1)}, bf16[96]{0:T(256)(128)(2,1)}, u32[]{:S(2)}) copy-start(bf16[96]{0:T(256)(128)(2,1)} %param.35) | copy-start | bytes 580
  8.0 14.3 %copy-start.58 = (bf16[96]{0:T(256)(128)(2,1)S(1)}, bf16[96]{0:T(256)(128)(2,1)}, u32[]{:S(2)}) copy-start(bf16[96]{0:T(256)(128)(2,1)} %param.38) | copy-start | bytes 580
  8.0 52.5 %copy-start.59 = (s32[8]{0:T(128)S(1)}, s32[8]{0:T(128)}, u32[]{:S(2)}) copy-start(s32[8]{0:T(128)} %param.33) | copy-start | bytes 100
  8.0 188.2 %all-gather.11.cloned.1.call-start = ((), (), s32[]{:S(2)}) async-start(), calls=%async_computation.15 | async-start | bytes 5308416 | tf_op jit(solution)/shard_map/all_gather | solution.py:150
  8.7 220.4 %all-gather.7.cloned.1.call-start = ((), (), s32[]{:S(2)}) async-start(), calls=%async_computation.13 | async-start | bytes 1327104 | tf_op jit(solution)/shard_map/all_gather | solution.py:147
  12.9 50.2 %all-to-all-start = ((bf16[64,8,1,768]{3,0,2,1:T(8,128)(2,1)}), bf16[64,8,1,768]{3,0,2,1:T(8,128)(2,1)S(1)}, u32[]{:S(2)}, u32[]{:S(2)}) async-start(bf16[64,8,1,768]{3,0,2,1:T(8,128)(2,1)} %copy.171), calls=%async_computation | async-start | bytes 1572864 | tf_op jit(solution)/shard_map/all_to_all | solution.py:131
  20.2 289.0 %all-gather.9.cloned.1.call-start = ((), (), s32[]{:S(2)}) async-start(), calls=%async_computation.14 | async-start | bytes 5308416 | tf_op jit(solution)/shard_map/all_gather | solution.py:149
  60.5 36.7 %copy-start.42 = (f32[768]{0:T(1024)}, f32[768]{0:T(1024)S(1)}, u32[]{:S(2)}) copy-start(f32[768]{0:T(1024)S(1)} %convert_element_type.196) | copy-start | bytes 9220
  63.1 166.0 %copy-start.6 = (bf16[64,8,1,768]{3,0,2,1:T(8,128)(2,1)}, bf16[64,8,1,768]{3,0,2,1:T(8,128)(2,1)S(1)}, u32[]{:S(2)}) copy-start(bf16[64,8,1,768]{3,0,2,1:T(8,128)(2,1)S(1)} %all-to-all-done) | copy-start | bytes 2359300
  63.3 34.0 %copy-start.44 = (f32[8,64]{1,0:T(8,128)}, f32[8,64]{1,0:T(8,128)S(1)}, u32[]{:S(2)}) copy-start(f32[8,64]{1,0:T(8,128)S(1)} %broadcast_multiply_fusion) | copy-start | bytes 6148
  63.3 33.9 %copy-start.46 = (f32[512]{0:T(512)}, f32[512]{0:T(512)S(1)}, u32[]{:S(2)}) copy-start(f32[512]{0:T(512)S(1)} %div.43) | copy-start | bytes 6148
  101.8 5.3 copy-start.40
  101.8 33.2 %all-to-all-start.1 = ((bf16[512,1,3,4,192]{0,4,2,1,3:T(8,128)(2,1)}), bf16[512,1,3,4,192]{0,4,2,1,3:T(8,128)(2,1)}, u32[]{:S(2)}, u32[]{:S(2)}) async-start(bf16[512,1,3,4,192]{0,4,2,1,3:T(8,128)(2,1)} %copy.178), calls=%async_computation.1 | async-start | bytes 4718592 | tf_op jit(solution)/shard_map/all_to_all | solution.py:159
  108.7 53.7 %copy-start.30 = (pred[512,1024]{1,0:T(8,128)(4,1)}, pred[512,1024]{1,0:T(8,128)(4,1)S(1)}, u32[]{:S(2)}) copy-start(pred[512,1024]{1,0:T(8,128)(4,1)S(1)} %fusion.26) | copy-start | bytes 1572868
  109.3 60.9 %copy-start.24 = (pred[512,1536]{1,0:T(8,128)(4,1)}, pred[512,1536]{1,0:T(8,128)(4,1)S(1)}, u32[]{:S(2)}) copy-start(pred[512,1536]{1,0:T(8,128)(4,1)S(1)} %fusion.14) | copy-start | bytes 2359300
  110.1 264.2 %copy-start.12 = (pred[512,2048]{1,0:T(8,128)(4,1)}, pred[512,2048]{1,0:T(8,128)(4,1)S(1)}, u32[]{:S(2)}) copy-start(pred[512,2048]{1,0:T(8,128)(4,1)S(1)} %fusion.12) | copy-start | bytes 3145732
  135.0 57.4 %all-to-all-start.4 = ((bf16[64,8,1,768]{3,0,2,1:T(8,128)(2,1)}), bf16[64,8,1,768]{3,0,2,1:T(8,128)(2,1)}, u32[]{:S(2)}, u32[]{:S(2)}) async-start(bf16[64,8,1,768]{3,0,2,1:T(8,128)(2,1)} %bitcast.314), calls=%async_computation.4 | async-start | bytes 1572864 | tf_op jit(solution)/shard_map/all_to_all | solution.py:134
  152.5 9.0 copy-start.9
  153.9 8.6 copy-start.4
  158.5 11.7 %copy-start.2 = (f32[3,512,1536]{2,1,0:T(8,128)}, f32[3,512,1536]{2,1,0:T(8,128)S(1)}, u32[]{:S(2)}) copy-start(f32[3,512,1536]{2,1,0:T(8,128)S(1)} %get-tuple-element.284) | copy-start | bytes 28311556
  192.4 15.3 %all-to-all-start.2 = ((bf16[4,2,49152]{2,1,0:T(2,128)(2,1)}), bf16[4,2,49152]{2,1,0:T(2,128)(2,1)S(1)}, u32[]{:S(2)}, u32[]{:S(2)}) async-start(bf16[4,2,49152]{2,1,0:T(2,128)(2,1)} %reshape.802), calls=%async_computation.2 | async-start | bytes 1572864 | tf_op jit(solution)/shard_map/all_to_all | solution.py:175
  233.0 89.1 %copy-start.21 = (f32[512,768]{1,0:T(8,128)S(1)}, f32[512,768]{1,0:T(8,128)}, u32[]{:S(2)}) copy-start(f32[512,768]{1,0:T(8,128)} %copy-done.20) | copy-start | bytes 4718596
  309.2 12.9 %copy-start.55 = (bf16[768,3072]{1,0:T(8,128)(2,1)S(1)}, bf16[768,3072]{1,0:T(8,128)(2,1)}, u32[]{:S(2)}) copy-start(bf16[768,3072]{1,0:T(8,128)(2,1)} %all-gather.9.cloned.1.call-done) | copy-start | bytes 14155780
  328.2 8.7 copy-start.34
  332.2 15.9 %all-to-all-start.5 = ((bf16[512,1,4,192]{0,3,1,2:T(8,128)(2,1)}), bf16[512,1,4,192]{0,3,1,2:T(8,128)(2,1)}, u32[]{:S(2)}, u32[]{:S(2)}) async-start(bf16[512,1,4,192]{0,3,1,2:T(8,128)(2,1)} %bitcast.42), calls=%async_computation.5 | async-start | bytes 1572864 | tf_op jit(solution)/shard_map/all_to_all | solution.py:210
  336.4 273.0 %reduce-scatter.7.cloned.1.call-start = ((), (), s32[]{:S(2)}) async-start(), calls=%async_computation.17 | async-start | bytes 2654208 | tf_op jit(solution)/shard_map/reduce_scatter | solution.py:242
  339.1 17.1 %slice-start.17 = ((s8[6291456]{0:T(1024)(128)(4,1)}), s8[2097152]{0:T(1024)(128)(4,1)S(1)}, s32[]{:S(2)}) async-start(s8[6291456]{0:T(1024)(128)(4,1)} %bitcast.302), calls=%async_computation.38 | async-start | bytes 4194304
  350.2 13.8 %copy-start.39 = (bf16[1,512,1,1,192]{1,4,0,3,2:T(8,128)(2,1)}, bf16[1,512,1,1,192]{1,4,0,3,2:T(8,128)(2,1)S(1)}, u32[]{:S(2)}) copy-start(bf16[1,512,1,1,192]{1,4,0,3,2:T(8,128)(2,1)S(1)} %get-tuple-element.274) | copy-start | bytes 589828
  350.2 5.9 slice-start.18
  356.1 7.9 slice-start.6
  356.2 7.9 slice-start.7
  364.1 6.4 copy-start.26
  364.1 6.4 copy-start.37
  364.1 10.2 slice-start
  364.1 10.2 slice-start.1
  383.0 11.7 %copy-start.11 = (f32[3,512,512]{1,2,0:T(8,128)S(1)}, f32[3,512,512]{1,2,0:T(8,128)}, u32[]{:S(2)}) copy-start(f32[3,512,512]{1,2,0:T(8,128)} %copy-done.9) | copy-start | bytes 9437188
  394.7 5.2 slice-start.19
  394.7 5.2 slice-start.20
  399.8 8.8 slice-start.9
  399.9 8.7 slice-start.10
  399.9 8.7 slice-start.11
  403.8 19.4 %slice-start.12 = ((s8[12582912]{0:T(1024)(128)(4,1)}), s8[4194304]{0:T(1024)(128)(4,1)S(1)}, s32[]{:S(2)}) async-start(s8[12582912]{0:T(1024)(128)(4,1)} %bitcast.298), calls=%async_computation.33 | async-start | bytes 8388608
  408.6 14.7 %slice-start.3 = ((s8[12582912]{0:T(1024)(128)(4,1)}), s8[4194304]{0:T(1024)(128)(4,1)S(1)}, s32[]{:S(2)}) async-start(s8[12582912]{0:T(1024)(128)(4,1)} %bitcast.292), calls=%async_computation.24 | async-start | bytes 8388608
  408.6 14.7 %slice-start.4 = ((s8[12582912]{0:T(1024)(128)(4,1)}), s8[4194304]{0:T(1024)(128)(4,1)S(1)}, s32[]{:S(2)}) async-start(s8[12582912]{0:T(1024)(128)(4,1)} %bitcast.292), calls=%async_computation.25 | async-start | bytes 8388608
  408.6 14.7 %slice-start.5 = ((s8[12582912]{0:T(1024)(128)(4,1)}), s8[4194304]{0:T(1024)(128)(4,1)S(1)}, s32[]{:S(2)}) async-start(s8[12582912]{0:T(1024)(128)(4,1)} %bitcast.292), calls=%async_computation.26 | async-start | bytes 8388608
  408.6 14.7 %slice-start.13 = ((s8[12582912]{0:T(1024)(128)(4,1)}), s8[4194304]{0:T(1024)(128)(4,1)S(1)}, s32[]{:S(2)}) async-start(s8[12582912]{0:T(1024)(128)(4,1)} %bitcast.298), calls=%async_computation.34 | async-start | bytes 8388608
  408.6 14.7 %slice-start.14 = ((s8[12582912]{0:T(1024)(128)(4,1)}), s8[4194304]{0:T(1024)(128)(4,1)S(1)}, s32[]{:S(2)}) async-start(s8[12582912]{0:T(1024)(128)(4,1)} %bitcast.298), calls=%async_computation.35 | async-start | bytes 8388608
  417.7 5.7 copy-start.13
  430.0 11.9 %slice-start.15 = ((s8[6291456]{0:T(1024)(128)(4,1)}), s8[2097152]{0:T(1024)(128)(4,1)S(1)}, s32[]{:S(2)}) async-start(s8[6291456]{0:T(1024)(128)(4,1)} %bitcast.300), calls=%async_computation.36 | async-start | bytes 4194304
  433.9 5.3 copy-start.5
  436.0 5.9 slice-start.16
  459.3 53.2 %all-to-all-start.6 = ((bf16[2048,1,3,1,192]{4,2,3,1,0:T(4,128)(2,1)}), bf16[2048,1,3,1,192]{4,2,3,1,0:T(4,128)(2,1)}, u32[]{:S(2)}, u32[]{:S(2)}) async-start(bf16[2048,1,3,1,192]{4,2,3,1,0:T(4,128)(2,1)} %pad_maximum_fusion), calls=%async_computation.6 | async-start | bytes 8388608 | tf_op jit(solution)/shard_map/all_to_all | solution.py:224
  464.3 217.2 %reduce-scatter.5.cloned.1.call-start = ((), (), s32[]{:S(2)}) async-start(), calls=%async_computation.16 | async-start | bytes 7962624 | tf_op jit(solution)/shard_map/reduce_scatter | solution.py:241
  526.7 319.6 %reduce-scatter.9.cloned.1.call-start = ((), (), s32[]{:S(2)}) async-start(), calls=%async_computation.18 | async-start | bytes 10616832 | tf_op jit(solution)/shard_map/reduce_scatter | solution.py:244
  535.3 475.9 %reduce-scatter.11.cloned.1.call-start = ((), (), s32[]{:S(2)}) async-start(), calls=%async_computation.19 | async-start | bytes 10616832 | tf_op jit(solution)/shard_map/reduce_scatter | solution.py:245
  554.4 10.6 copy-start.28
  554.4 10.6 copy-start.47
  560.6 45.3 %all-to-all-start.3 = ((bf16[8,2,24576]{2,1,0:T(2,128)(2,1)}), bf16[8,2,24576]{2,1,0:T(2,128)(2,1)}, u32[]{:S(2)}, u32[]{:S(2)}) async-start(bf16[8,2,24576]{2,1,0:T(2,128)(2,1)} %reshape.804), calls=%async_computation.3 | async-start | bytes 1572864 | tf_op jit(solution)/shard_map/all_to_all | solution.py:187
  605.8 440.2 %all-to-all-start.7 = ((bf16[8,2,24576]{2,1,0:T(2,128)(2,1)}), bf16[8,2,24576]{2,1,0:T(2,128)(2,1)S(1)}, u32[]{:S(2)}, u32[]{:S(2)}) async-start(bf16[8,2,24576]{2,1,0:T(2,128)(2,1)} %reshape.806), calls=%async_computation.7 | async-start | bytes 1572864 | tf_op jit(solution)/shard_map/all_to_all | solution.py:232
  609.4 476.8 %all-reduce.12.cloned.1.call-start = ((), (), s32[]{:S(2)}) async-start(), calls=%async_computation.20 | async-start | bytes 3538944 | tf_op jit(solution)/shard_map/psum | solution.py:249
  1047.0 46.2 %copy-start.1 = (bf16[5,768]{1,0:T(8,128)(2,1)S(1)}, bf16[5,768]{1,0:T(8,128)(2,1)}, u32[]{:S(2)}) copy-start(bf16[5,768]{1,0:T(8,128)(2,1)} %param.34) | copy-start | bytes 23044
  1086.2 5.9 copy-start.41
  (34 other events, 99.8 us)
Sparse Core Ops, SparseCore 0:
  10.2 81.6 all-gather.4
  94.0 92.6 all-gather.10
  188.9 40.0 all-gather.6
  231.1 78.0 all-gather.8
  340.4 68.8 reduce-scatter.6
  526.8 154.6 reduce-scatter.4
  685.1 161.2 reduce-scatter.8
  849.9 161.2 reduce-scatter.10
  1014.9 45.7 all-reduce.11
where the time goes:
time: 1110 us; the launch traced here: 1100 us
  waiting for transfers between devices  626 us (56%)
  matrix products  157 us (14%)
  blocking collectives  101 us (9%)
  local copies, waits for them, and re-layouts  83.1 us (7%)
  other arithmetic  77.9 us (7%)
  starting transfers between devices  38.7 us (3%)
  between operations  16.7 us (2%)
    reduce_scatter x1, waiting for transfers between devices, per_device(): lax.psum_scatter(grad_up, 'fsdp', scatter_dimension=0, tiled=True)  163 us
    reduce_scatter x1, waiting for transfers between devices, per_device(): lax.psum_scatter(grad_down, 'fsdp', scatter_dimension=0, tiled=True)  163 us
    all_gather x1, waiting for transfers between devices, per_device(): lax.all_gather(shard_set[4], 'fsdp', axis=0, tiled=True)  76.2 us
    reduce_scatter x1, waiting for transfers between devices, per_device(): lax.psum_scatter(grad_qkv, 'fsdp', scatter_dimension=0, tiled=True)  70.3 us
    unnamed x2, blocking collectives  57.7 us
    all_to_all x1, waiting for transfers between devices, per_device(): lax.all_to_all(as_sent(d_parts), 'seq', split_axis=0, concat_axis=3, tile...  46.9 us
    psum x1, blocking collectives, per_device(): grad_table = lax.psum(grad_table, ('seq', 'fsdp'))  37.7 us
    all_to_all x1, waiting for transfers between devices, per_device(): lax.all_to_all(result.reshape(return_shape), 'fsdp', split_axis=0, concat...  31 us
  transfers between devices with their start and end apart: 17, of which 11 were waited for; matrix products, arithmetic and copies ran while one was open for 25% of the time, Pallas kernels for 0%

commit v1 on v0

v1 whole, which is shorter than its diff:
```python
import functools

import jax
import jax.numpy as jnp
from jax import lax
from jax.experimental import pallas as pl
from jax.experimental.pallas import tpu as pltpu
from jax.sharding import PartitionSpec as P

HEADS = 12
EPSILON = 1e-05
LOG2E = 1.4426950408889634
LN2 = 0.6931471805599453
MASKED = -1e30
DH = 64


def dotg(a, b, ca, cb):
    return lax.dot_general(a, b, (((ca,), (cb,)), ((), ())), preferred_element_type=jnp.float32)


def attend_body(info, qkv, out, lse, acc, *, heads, blk):
    h = pl.program_id(0)
    i = pl.program_id(1)
    me = info[0]
    length = info[1]
    qt = qkv[i ^ me, pl.ds(pl.multiple_of(h * DH, DH), DH), :]
    scale = DH ** -0.5 * LOG2E

    def step(j, carry, masked):
        top, tot = carry
        kt = qkv[j ^ me, pl.ds(pl.multiple_of((heads + h) * DH, DH), DH), :]
        vt = qkv[j ^ me, pl.ds(pl.multiple_of((2 * heads + h) * DH, DH), DH), :]
        st = dotg(kt, qt, 0, 0) * scale
        if masked:
            key_at = j * blk + lax.broadcasted_iota(jnp.int32, st.shape, 0)
            query_at = i * blk + lax.broadcasted_iota(jnp.int32, st.shape, 1)
            st = jnp.where((query_at >= key_at) & (key_at < length), st, MASKED)
        new_top = jnp.maximum(top, jnp.max(st, axis=0, keepdims=True))
        fade = jnp.exp2(top - new_top)
        pt = jnp.exp2(st - new_top)
        tot = tot * fade + jnp.sum(pt, axis=0, keepdims=True)
        acc[...] = acc[...] * fade + dotg(vt, pt.astype(jnp.bfloat16), 1, 0)
        return new_top, tot

    acc[...] = jnp.zeros_like(acc)
    carry = (jnp.full((1, blk), MASKED, jnp.float32), jnp.zeros((1, blk), jnp.float32))
    plain = jnp.minimum(i, length // blk)
    stop = jnp.minimum(i + 1, (length + blk - 1) // blk)
    carry = lax.fori_loop(0, plain, functools.partial(step, masked=False), carry)
    top, tot = lax.fori_loop(plain, stop, functools.partial(step, masked=True), carry)
    out[0] = (acc[...] / tot).astype(jnp.bfloat16)
    lse[0, 0] = top + jnp.log2(tot)


def attend(info, qkv, heads):
    blocks, _, blk = qkv.shape
    flops = 2 * 2 * heads * DH * (blocks * blk) ** 2 // 2
    return pl.pallas_call(
        functools.partial(attend_body, heads=heads, blk=blk),
        grid_spec=pltpu.PrefetchScalarGridSpec(
            num_scalar_prefetch=1,
            grid=(heads, blocks),
            in_specs=[pl.BlockSpec(qkv.shape, lambda h, i, info: (0, 0, 0))],
            out_specs=[
                pl.BlockSpec((1, DH, blk), lambda h, i, info: (i, h, 0)),
                pl.BlockSpec((1, 1, 1, blk), lambda h, i, info: (h, i, 0, 0)),
            ],
            scratch_shapes=[pltpu.VMEM((DH, blk), jnp.float32)],
        ),
        out_shape=[
            jax.ShapeDtypeStruct((blocks, heads * DH, blk), jnp.bfloat16),
            jax.ShapeDtypeStruct((heads, blocks, 1, blk), jnp.float32),
        ],
        cost_estimate=pl.CostEstimate(flops=4 * flops, bytes_accessed=4 * qkv.size, transcendentals=0),
        name="attend",
    )(info, qkv)


def attend_back_body(info, qkv, att, datt, lse, dqkv, dq, q_rows, do_rows, delta, *, heads, blocks, blk):
    h = pl.program_id(0)
    j = pl.program_id(1)
    me = info[0]
    length = info[1]
    scale = DH ** -0.5
    at_q = pl.ds(pl.multiple_of(h * DH, DH), DH)
    at_k = pl.ds(pl.multiple_of((heads + h) * DH, DH), DH)
    at_v = pl.ds(pl.multiple_of((2 * heads + h) * DH, DH), DH)

    @pl.when(j == 0)
    def _():
        dq[...] = jnp.zeros_like(dq)
        for b in range(blocks):
            dt = datt[b, at_q, :]
            q_rows[b] = qkv[b ^ me, at_q, :].T
            do_rows[b] = dt.T
            delta[b] = jnp.sum(dt.astype(jnp.float32) * att[b, at_q, :].astype(jnp.float32), axis=0, keepdims=True)

    kt = qkv[j ^ me, at_k, :]
    vt = qkv[j ^ me, at_v, :]
    k_rows = kt.T
    v_rows = vt.T

    def step(i, carry, masked):
        dk, dv = carry
        qt = qkv[i ^ me, at_q, :]
        st = jnp.dot(k_rows, qt, preferred_element_type=jnp.float32)
        pt = jnp.exp2(st * (scale * LOG2E) - lse[0, i])
        if masked:
            key_at = j * blk + lax.broadcasted_iota(jnp.int32, st.shape, 0)
            query_at = i * blk + lax.broadcasted_iota(jnp.int32, st.shape, 1)
            pt = jnp.where((query_at >= key_at) & (key_at < length), pt, 0.0)
        dpt = jnp.dot(v_rows, datt[i, at_q, :], preferred_element_type=jnp.float32)
        dst = (pt * (dpt - delta[i])).astype(jnp.bfloat16)
        dv = dv + jnp.dot(pt.astype(jnp.bfloat16), do_rows[i], preferred_element_type=jnp.float32)
        dk = dk + jnp.dot(dst, q_rows[i], preferred_element_type=jnp.float32)
        dq[i] = dq[i] + jnp.dot(kt, dst, preferred_element_type=jnp.float32)
        return dk, dv

    zero = jnp.zeros((blk, DH), jnp.float32)
    whole = (j + 1) * blk <= length
    some = j * blk < length
    masked_end = jnp.where(some, jnp.where(whole, j + 1, blocks), j)
    carry = lax.fori_loop(j, masked_end, functools.partial(step, masked=True), (zero, zero))
    dk, dv = lax.fori_loop(
        jnp.where(whole, j + 1, blocks), blocks, functools.partial(step, masked=False), carry
    )
    dqkv[j ^ me, at_k, :] = (dk * scale).astype(jnp.bfloat16).T
    dqkv[j ^ me, at_v, :] = dv.astype(jnp.bfloat16).T
    dqkv[j ^ me, at_q, :] = (dq[j] * scale).astype(jnp.bfloat16)


def attend_back(info, qkv, att, datt, lse, heads):
    blocks, _, blk = qkv.shape
    flops = 5 * 2 * heads * DH * (blocks * blk) ** 2 // 2
    whole = lambda a: pl.BlockSpec(a.shape, lambda h, j, info: (0,) * a.ndim)
    return pl.pallas_call(
        functools.partial(attend_back_body, heads=heads, blocks=blocks, blk=blk),
        grid_spec=pltpu.PrefetchScalarGridSpec(
            num_scalar_prefetch=1,
            grid=(heads, blocks),
            in_specs=[
                whole(qkv),
                whole(att),
                whole(datt),
                pl.BlockSpec((1, blocks, 1, blk), lambda h, j, info: (h, 0, 0, 0)),
            ],
            out_specs=whole(qkv),
            scratch_shapes=[
                pltpu.VMEM((blocks, DH, blk), jnp.float32),
                pltpu.VMEM((blocks, blk, DH), jnp.bfloat16),
                pltpu.VMEM((blocks, blk, DH), jnp.bfloat16),
                pltpu.VMEM((blocks, 1, blk), jnp.float32),
            ],
        ),
        out_shape=jax.ShapeDtypeStruct(qkv.shape, jnp.bfloat16),
        cost_estimate=pl.CostEstimate(flops=4 * flops, bytes_accessed=8 * qkv.size, transcendentals=0),
        name="attend_back",
    )(info, qkv, att, datt, lse)


GELU_A = 0.7978845608028654
GELU_B = 0.044715


def mlp_body(nm, cot, wu, wd, acc_in, dnm_in, acc, dnm, dwu, dwd):
    @pl.when(pl.program_id(0) == 0)
    def _():
        acc[...] = acc_in[...]
        dnm[...] = dnm_in[...]

    x = nm[...]
    g = cot[...]
    u = jnp.dot(x, wu[...], preferred_element_type=jnp.float32)
    da = dotg(g, wd[...], 1, 1)
    square = u * u
    th = jnp.tanh(GELU_A * u * (1.0 + GELU_B * square))
    half = 0.5 * (1.0 + th)
    a = (u * half).astype(jnp.bfloat16)
    slope = half + 0.5 * u * (1.0 - th * th) * (GELU_A * (1.0 + 3.0 * GELU_B * square))
    du = (da * slope).astype(jnp.bfloat16)
    acc[...] += jnp.dot(a, wd[...], preferred_element_type=jnp.float32)
    dnm[...] += dotg(du, wu[...], 1, 1)
    dwd[...] = dotg(a, g, 0, 0).astype(jnp.bfloat16)
    dwu[...] = dotg(x, du, 0, 0).astype(jnp.bfloat16)


def mlp_part(nm, cot, wu, wd, acc, dnm, step=256):
    rows, width = nm.shape
    ff = wu.shape[1]
    whole = pl.BlockSpec((rows, width), lambda i: (0, 0))
    up = pl.BlockSpec((width, step), lambda i: (0, i))
    down = pl.BlockSpec((step, width), lambda i: (i, 0))
    return pl.pallas_call(
        mlp_body,
        grid=(ff // step,),
        in_specs=[whole, whole, up, down, whole, whole],
        out_specs=[whole, whole, up, down],
        out_shape=[
            jax.ShapeDtypeStruct((rows, width), jnp.float32),
            jax.ShapeDtypeStruct((rows, width), jnp.float32),
            jax.ShapeDtypeStruct(wu.shape, jnp.bfloat16),
            jax.ShapeDtypeStruct(wd.shape, jnp.bfloat16),
        ],
        input_output_aliases={4: 0, 5: 1},
        cost_estimate=pl.CostEstimate(flops=12 * rows * width * ff, bytes_accessed=8 * width * ff, transcendentals=0),
        name="mlp_part",
    )(nm, cot, wu, wd, acc, dnm)


def swap(value, axis, bit):
    count = lax.axis_size(axis)
    return lax.ppermute(value, axis, [(i, i ^ bit) for i in range(count)])


def bits_of(axis):
    count = lax.axis_size(axis)
    assert count & (count - 1) == 0, "axis size"
    return [1 << b for b in reversed(range(count.bit_length() - 1))]


def is_set(axis, bit):
    return (lax.axis_index(axis) & bit) != 0


def join(own, came, axis, bit, at):
    high = is_set(axis, bit)
    return jnp.stack((jnp.where(high, came, own), jnp.where(high, own, came)), axis=at)


def gather(value, axis, bits, at=0):
    for k, bit in enumerate(bits):
        value = join(value, swap(value, axis, bit), axis, bit, at + k)
    return value


def spread(blocks, bit):
    return blocks | {r ^ bit: swap(b, "seq", bit) for r, b in blocks.items()}


def add(a, b):
    return (a.astype(jnp.float32) + b.astype(jnp.float32)).astype(a.dtype)


def fold(blocks, bit):
    return {r: add(b, swap(blocks[r ^ bit], "seq", bit)) for r, b in blocks.items() if not r & bit}


def halve(value, axis, bit, at):
    mine = is_set(axis, bit).astype(jnp.int32)
    keep = lax.dynamic_index_in_dim(value, mine, at, keepdims=False)
    give = lax.dynamic_index_in_dim(value, 1 - mine, at, keepdims=False)
    return add(keep, swap(give, axis, bit))


def norm_stats(values):
    centre = jnp.mean(values, axis=-1, keepdims=True)
    shifted = values - centre
    spread_of = jnp.mean(shifted * shifted, axis=-1, keepdims=True)
    inverse = lax.rsqrt(spread_of + EPSILON)
    return shifted * inverse, inverse


def norm_back(z, inverse, gain, grad):
    e = grad * gain
    back = (e - jnp.mean(e, axis=-1, keepdims=True) - z * jnp.mean(e * z, axis=-1, keepdims=True)) * inverse
    return back, jnp.sum(grad * z, axis=0, keepdims=True)


def per_device(
    tokens, pass_index, lengths, table, gain_attn, w_qkv, w_out, gain_mlp, w_up, w_down, cotangent
):
    bf16, f32 = jnp.bfloat16, jnp.float32
    groups, parts = lax.axis_size("fsdp"), lax.axis_size("seq")
    local_len, seq_total, width = tokens.shape
    assert seq_total == groups
    heads = HEADS // parts
    part = width // parts
    ff = w_up.shape[1]
    own_rows = width // groups
    me, group = lax.axis_index("seq"), lax.axis_index("fsdp")
    f_bits, s_bits = bits_of("fsdp"), bits_of("seq")
    span = local_len * groups
    pick = lambda a, at: lax.dynamic_index_in_dim(a, me, at, keepdims=False)

    qkv_slice = pick(w_qkv.reshape(own_rows, 3, parts, part), 2).reshape(own_rows, 3 * part)
    gains = jnp.stack((gain_attn, gain_mlp), axis=1)
    qkv_slice = jnp.concatenate(
        (qkv_slice, gains, jnp.zeros((own_rows, -(3 * part + 2) % 128), bf16)), axis=1
    )
    ff_each = ff // groups // parts
    up_slice = pick(w_up.reshape(own_rows, groups, parts, ff_each), 2).reshape(own_rows, ff // parts)
    down_slice = pick(w_down.reshape(parts, ff_each, width), 0)
    out_slice = pick(w_out.reshape(parts, own_rows // parts, width), 0)

    chooser = (pass_index[..., None] == jnp.arange(table.shape[0], dtype=jnp.int32)).astype(bf16)
    embedded = jnp.einsum("pnc,cd->npd", chooser, table, preferred_element_type=f32)
    summed = (jnp.swapaxes(tokens, 0, 1).astype(f32) + embedded).astype(bf16)
    deal = lambda a: lax.all_to_all(a, "fsdp", split_axis=0, concat_axis=0, tiled=True)
    inputs = deal(summed).reshape(span, width)
    qkv_full = gather(qkv_slice, "fsdp", f_bits).reshape(width, -1)
    wq = qkv_full[:, : 3 * part]
    gain_one = qkv_full[:, 3 * part].astype(f32)
    gain_two = qkv_full[:, 3 * part + 1].astype(f32)
    cot = deal(jnp.swapaxes(cotangent, 0, 1)).reshape(span, width)
    passes = lax.dynamic_index_in_dim(gather(pass_index, "fsdp", f_bits), group, -1, keepdims=False).reshape(span)

    up_all = {0: gather(up_slice, "fsdp", f_bits).reshape(width, ff // parts)}
    for bit in s_bits:
        up_all = spread(up_all, bit)
    down_all = {0: gather(down_slice, "fsdp", f_bits[:-1])}
    for bit in s_bits[:-1]:
        down_all = spread(down_all, bit)
    down_all = {
        r: join(b, swap(b, "fsdp", f_bits[-1]), "fsdp", f_bits[-1], len(f_bits) - 1).reshape(ff // parts, width)
        for r, b in down_all.items()
    }
    down_all = spread(down_all, s_bits[-1])
    w_out_full = gather(gather(out_slice, "fsdp", f_bits), "seq", s_bits, len(f_bits)).reshape(width, width)

    rows = {0: inputs}
    for bit in s_bits:
        rows = spread(rows, bit)
    normed, inverse_one, z_one = {}, None, None
    pieces = []
    for r in range(parts):
        z, inverse = norm_stats(rows[r].astype(f32))
        normed[r] = (z * gain_one).astype(bf16)
        pieces.append(dotg(wq, normed[r], 0, 1).astype(bf16))
    qkv = jnp.stack(pieces)
    info = jnp.stack((me, lax.dynamic_index_in_dim(lengths, group, 0, keepdims=False))).astype(jnp.int32)
    att_heads, lse = attend(info, qkv, heads)
    across = lambda a: lax.all_to_all(a, "seq", split_axis=0, concat_axis=0, tiled=True)
    att = across(att_heads).reshape(width, span)

    residual = inputs.astype(f32) + dotg(att, w_out_full, 0, 0)
    z_two, inverse_two = norm_stats(residual)
    normed_mlp = (z_two * gain_two).astype(bf16)
    result = residual
    d_normed_mlp = jnp.zeros_like(residual)
    d_up, d_down = {}, {}
    for r in reversed(range(parts)):
        result, d_normed_mlp, d_up[r], d_down[r] = mlp_part(
            normed_mlp, cot, up_all[r], down_all[r], result, d_normed_mlp
        )
    out_back = deal(result.astype(bf16).reshape(groups, local_len, width))
    d_res_norm, d_gain_mlp = norm_back(z_two, inverse_two, gain_two, d_normed_mlp)
    d_residual = cot.astype(f32) + d_res_norm
    d_branch = d_residual.astype(bf16)
    d_att = dotg(w_out_full, d_branch, 1, 1).astype(bf16)
    d_heads = across(d_att.reshape(parts, part, span))

    sizes = (2,) * len(f_bits)
    for bit in reversed(s_bits):
        d_up = fold(d_up, bit)
    d_up = d_up[0].reshape(*sizes, own_rows, ff // parts)
    for k in reversed(range(len(f_bits))):
        d_up = halve(d_up, "fsdp", f_bits[k], k)
    d_down = {r: b.reshape(*sizes, ff_each, width) for r, b in fold(d_down, s_bits[-1]).items()}
    last = len(f_bits) - 1
    d_down = {r: halve(b, "fsdp", f_bits[last], last) for r, b in d_down.items()}
    for bit in reversed(s_bits[:-1]):
        d_down = fold(d_down, bit)
    d_down = d_down[0]
    for k in reversed(range(last)):
        d_down = halve(d_down, "fsdp", f_bits[k], k)
    d_out = dotg(att, d_branch, 0 + 1, 0).astype(bf16)
    d_out = d_out.reshape(*sizes, *(2,) * len(s_bits), own_rows // parts, width)
    for k in reversed(range(len(s_bits))):
        d_out = halve(d_out, "seq", s_bits[k], len(f_bits) + k)
    for k in reversed(range(len(f_bits))):
        d_out = halve(d_out, "fsdp", f_bits[k], k)

    d_qkv = attend_back(info, qkv, att_heads, d_heads, lse, heads)
    d_rows = {r: dotg(d_qkv[r], wq, 0, 1).astype(bf16) for r in range(parts)}
    for bit in reversed(s_bits[1:]):
        d_rows = fold(d_rows, bit)
    d_normed = d_rows[0].astype(f32) + swap(d_rows[s_bits[0]], "seq", s_bits[0]).astype(f32)
    z_one, inverse_one = norm_stats(inputs.astype(f32))
    d_in_norm, d_gain_attn = norm_back(z_one, inverse_one, gain_one, d_normed)
    d_inputs = (d_residual + d_in_norm).astype(bf16)
    d_back = deal(d_inputs.reshape(groups, local_len, width))
    d_wq = sum(dotg(normed[r], d_qkv[r], 0, 1) for r in range(parts)).astype(bf16)
    d_wq = d_wq.reshape(*sizes, own_rows, 3 * part)
    for k in reversed(range(len(f_bits))):
        d_wq = halve(d_wq, "fsdp", f_bits[k], k)

    picks = (passes[None, :] == jnp.arange(table.shape[0], dtype=jnp.int32)[:, None]).astype(bf16)
    d_table = jnp.dot(picks, d_inputs, preferred_element_type=f32)
    small = jnp.concatenate((d_table, d_gain_attn, d_gain_mlp, jnp.zeros_like(d_gain_mlp)), axis=0)
    for bit in reversed(s_bits):
        small = small + swap(small, "seq", bit)
    for bit in reversed(f_bits):
        small = small + swap(small, "fsdp", bit)
    owned_gain = lambda row: lax.dynamic_slice_in_dim(small[row], group * own_rows, own_rows)

    whole = lambda a: gather(a, "seq", s_bits).reshape(parts, *a.shape).astype(f32)
    g_qkv = whole(d_wq).reshape(parts, own_rows, 3, part).transpose(1, 2, 0, 3).reshape(own_rows, 3 * width)
    g_up = whole(d_up).reshape(parts, own_rows, groups, ff_each).transpose(1, 2, 0, 3).reshape(own_rows, ff)
    g_down = whole(d_down).reshape(ff // groups, width)
    g_out = whole(d_out).reshape(own_rows, width)
    count = table.shape[0]
    return (
        jnp.swapaxes(out_back, 0, 1),
        jnp.swapaxes(d_back, 0, 1),
        small[:count],
        owned_gain(count),
        g_qkv,
        g_out,
        owned_gain(count + 1),
        g_up,
        g_down,
    )


def solution(mesh):
    return jax.shard_map(
        per_device,
        mesh=mesh,
        in_specs=(
            P(("seq", "fsdp"), None, None),
            P(("seq", "fsdp"), None),
            P(),
            P(),
            P("fsdp"),
            P("fsdp", None),
            P("fsdp", None),
            P("fsdp"),
            P("fsdp", None),
            P("fsdp", None),
            P(("seq", "fsdp"), None, None),
        ),
        out_specs=(
            P(("seq", "fsdp"), None, None),
            P(("seq", "fsdp"), None, None),
            P(),
            P("fsdp"),
            P("fsdp", None),
            P("fsdp", None),
            P("fsdp"),
            P("fsdp", None),
            P("fsdp", None),
        ),
        check_vma=False,
    )
```

time: 1110 us -> 514 us (0.46)
  waiting for transfers between devices: 626 us -> 200 us
  matrix products: 157 us -> 22 us
  blocking collectives: 101 us -> 0 us
  Pallas kernels: 0 us -> 92.6 us
  starting transfers between devices: 38.7 us -> 100 us
  local copies, waits for them, and re-layouts: 83.1 us -> 42.9 us
  other arithmetic: 77.9 us -> 48.9 us
  between operations: 16.7 us -> 2.38 us
    reduce_scatter x4 -> x0, waiting for transfers between devices: 396 us -> none  [the longest x1 163 us: per_device(): lax.psum_scatter(grad_up, 'fsdp', scatter_dimension=0, tiled=True)]
    ppermute x0 -> x64, waiting for transfers between devices: none -> 174 us  [swap(): return lax.ppermute(value, axis, [(i, i ^ bit) for i in range(count)])]
    dot_general x38 -> x17, matrix products: 157 us -> 22 us  [the longest x15 20.2 us: dotg(): lax.dot_general(a, b, (((ca,), (cb,)), ((), ())), preferred_element_type=...]
    all_gather x4 -> x0, waiting for transfers between devices: 112 us -> none  [the longest x1 76.2 us: per_device(): lax.all_gather(shard_set[4], 'fsdp', axis=0, tiled=True)]
    pallas_call x0 -> x6, Pallas kernels: none -> 92.6 us  [the longest x4 37 us: mlp_part(): pl.pallas_call(mlp_body, grid=(ff // step,), in_specs=[whole, whole, up,...]
    all_to_all x8 -> x6, waiting for transfers between devices: 115 us -> 26.2 us  [the longest x4 13.6 us: per_device(): lax.all_to_all(a, 'fsdp', split_axis=0, concat_axis=0, tiled=True)]
    ppermute x0 -> x64, starting transfers between devices: none -> 71.9 us  [swap(): return lax.ppermute(value, axis, [(i, i ^ bit) for i in range(count)])]
    unnamed x2 -> x0, blocking collectives: 57.7 us -> none
  transfers between devices with their start and end apart: 17 -> 70, of which waited for: 11 -> 28; matrix products, arithmetic and copies ran while one was open for 25% -> 19% of each run, Pallas kernels for 0% -> 15%
where the time goes in v1:
time: 514 us; the launch traced here: 509 us
  waiting for transfers between devices  200 us (39%)
  starting transfers between devices  100 us (19%)
  Pallas kernels  92.6 us (18%)
  other arithmetic  48.9 us (10%)
  local copies, waits for them, and re-layouts  42.9 us (8%)
  matrix products  22 us (4%)
    ppermute x64, waiting for transfers between devices, swap(): return lax.ppermute(value, axis, [(i, i ^ bit) for i in range(count)])  174 us
    ppermute x64, starting transfers between devices, swap(): return lax.ppermute(value, axis, [(i, i ^ bit) for i in range(count)])  71.9 us
    pallas_call x4, Pallas kernels, mlp_part(): pl.pallas_call(mlp_body, grid=(ff // step,), in_specs=[whole, whole, up,...  37 us
    pallas_call x1, Pallas kernels, attend_back(): pl.pallas_call(functools.partial(attend_back_body, heads=heads, blocks=bl...  33.2 us
    pallas_call x1, Pallas kernels, attend(): pl.pallas_call(functools.partial(attend_body, heads=heads, blk=blk), grid...  22.4 us
    dot_general x15, matrix products, dotg(): lax.dot_general(a, b, (((ca,), (cb,)), ((), ())), preferred_element_type=...  20.2 us
    all_to_all x4, starting transfers between devices, per_device(): lax.all_to_all(a, 'fsdp', split_axis=0, concat_axis=0, tiled=True)  19.9 us
    another operation x48, other arithmetic, join(): jnp.stack((jnp.where(high, came, own), jnp.where(high, own, came)), axis=at)  19.2 us
  transfers between devices with their start and end apart: 70, of which 28 were waited for; matrix products, arithmetic and copies ran while one was open for 19% of the time, Pallas kernels for 15%

profile of v1, /device:TPU:0, one launch (start us, length us, event | category | flops | bytes accessed | tf_op | source)
XLA Modules:
  0.0 508.9 jit_solution(7444088581451903996)
XLA Ops:
  1.7 4.1 collective-permute-start.14
  5.8 2.3 reshape.287
  10.4 2.9 collective-permute-start.6
  14.8 2.9 collective-permute-start.27
  19.2 4.0 all-to-all-start
  23.8 6.5 %collective-permute-done.27 = s32[64,8]{0,1:T(8,128)S(1)} collective-permute-done((s32[64,8]{0,1:T(8,128)S(1)}, s32[64,8]{0,1:T(8,128)S(1)}, u32[]{:S(2)}, u32[]{:S(2)}) %collective-permute-start.27) | collective-permute-done | bytes 2080 | tf_op jit(solution)/shard_map/ppermute | solution.py:213
  30.3 6.9 %collective-permute-start.28 = (s32[2,64,8]{1,2,0:T(8,128)S(1)}, s32[2,64,8]{1,2,0:T(8,128)S(1)}, u32[]{:S(2)}, u32[]{:S(2)}) collective-permute-start(s32[2,64,8]{1,2,0:T(8,128)S(1)} %pad_add_fusion.1), channel_id=1, source_target_pairs={{0,2},{1,3},{2,0},{3,1},{4,6},{5,7},{6,4},{7,5},{8,10},{9,11},{10,... | collective-permute-start | bytes 12296 | tf_op jit(solution)/shard_map/ppermute | solution.py:213
  44.6 2.3 collective-permute-done.7
  55.4 3.4 collective-permute-done.1
  61.2 4.1 collective-permute-done.15
  74.6 2.1 copy.150
  81.0 14.8 %collective-permute-done.13 = bf16[2,2,96,768]{3,2,0,1:T(8,128)(2,1)} collective-permute-done((bf16[2,2,96,768]{3,2,0,1:T(8,128)(2,1)}, bf16[2,2,96,768]{3,2,0,1:T(8,128)(2,1)}, u32[]{:S(2)}, u32[]{:S(2)}) %collective-permute-start.13) | collective-permute-done | bytes 589856 | tf_op jit(solution)/shard_map/ppermute | solution.py:213
  103.4 2.1 fusion.34
  106.4 34.7 %collective-permute-done.4 = bf16[512,768]{1,0:T(8,128)(2,1)S(1)} collective-permute-done((bf16[512,768]{1,0:T(8,128)(2,1)S(1)}, bf16[512,768]{1,0:T(8,128)(2,1)S(1)}, u32[]{:S(2)}, u32[]{:S(2)}) %collective-permute-start.4) | collective-permute-done | bytes 786464 | tf_op jit(solution)/shard_map/ppermute | solution.py:213
  145.7 1.7 pad_maximum_fusion.qkv
  147.4 22.4 %attend.1 = (bf16[4,192,512]{2,1,0:T(8,128)(2,1)}, f32[3,4,1,512]{3,2,1,0:T(1,128)}) custom-call(s32[2]{0:T(128)} %pad_add_fusion.2.info, bf16[4,576,512]{2,1,0:T(8,128)(2,1)} %pad_maximum_fusion.qkv), custom_call_target="tpu_custom_call" | custom-call | flops 6442450944 | bytes 4718592 | tf_op jit(solution)/shard_map/attend/pallas_call | solution.py:59
  169.8 4.0 all-to-all-start.1
  177.5 8.0 %all-to-all-done.1 = bf16[4,192,512]{2,1,0:T(8,128)(2,1)S(1)} async-done(((bf16[4,192,512]{2,1,0:T(8,128)(2,1)}), bf16[4,192,512]{2,1,0:T(8,128)(2,1)S(1)}, u32[]{:S(2)}, u32[]{:S(2)}) %all-to-all-start.1) | async-done | bytes 786464 | tf_op jit(solution)/shard_map/all_to_all | solution.py:333
  185.4 8.4 %all-to-all-start.2 = ((bf16[8,64,768]{2,1,0:T(8,128)(2,1)}), bf16[8,64,768]{2,1,0:T(8,128)(2,1)}, u32[]{:S(2)}, u32[]{:S(2)}) async-start(bf16[8,64,768]{2,1,0:T(8,128)(2,1)} %bitcast.286), calls=%async_computation.2 | async-start | bytes 1572864 | tf_op jit(solution)/shard_map/all_to_all | solution.py:299
  195.6 2.0 fusion.85
  200.3 13.5 %all-to-all-done.2 = bf16[8,64,768]{2,1,0:T(8,128)(2,1)} async-done(((bf16[8,64,768]{2,1,0:T(8,128)(2,1)}), bf16[8,64,768]{2,1,0:T(8,128)(2,1)}, u32[]{:S(2)}, u32[]{:S(2)}) %all-to-all-start.2) | async-done | bytes 786464 | tf_op jit(solution)/shard_map/all_to_all | solution.py:299
  215.1 9.2 %mlp_part.4 = (f32[512,768]{1,0:T(8,128)}, f32[512,768]{1,0:T(8,128)}, bf16[768,768]{1,0:T(8,128)(2,1)}, bf16[768,768]{1,0:T(8,128)(2,1)}) custom-call(bf16[512,768]{1,0:T(8,128)(2,1)} %multiply_convert_fusion.nm, bf16[512,768]{1,0:T(8,128)(2,1)} %bitcast.37.cot, ...), custom_call_target="tpu_custom_call", output_to_operand_aliasing={{0}: (4, {}), {1}: (5, {})} | custom-call | flops 3623878656 | bytes 4718592 | tf_op jit(solution)/shard_map/mlp_part/pallas_call | solution.py:194
  224.3 9.2 %mlp_part.5 = (f32[512,768]{1,0:T(8,128)}, f32[512,768]{1,0:T(8,128)}, bf16[768,768]{1,0:T(8,128)(2,1)}, bf16[768,768]{1,0:T(8,128)(2,1)}) custom-call(bf16[512,768]{1,0:T(8,128)(2,1)} %multiply_convert_fusion.nm, bf16[512,768]{1,0:T(8,128)(2,1)} %bitcast.37.cot, ...), custom_call_target="tpu_custom_call", output_to_operand_aliasing={{0}: (4, {}), {1}: (5, {})} | custom-call | flops 3623878656 | bytes 4718592 | tf_op jit(solution)/shard_map/mlp_part/pallas_call | solution.py:194
  233.6 9.3 %mlp_part.6 = (f32[512,768]{1,0:T(8,128)}, f32[512,768]{1,0:T(8,128)}, bf16[768,768]{1,0:T(8,128)(2,1)}, bf16[768,768]{1,0:T(8,128)(2,1)}) custom-call(bf16[512,768]{1,0:T(8,128)(2,1)} %multiply_convert_fusion.nm, bf16[512,768]{1,0:T(8,128)(2,1)} %bitcast.37.cot, ...), custom_call_target="tpu_custom_call", output_to_operand_aliasing={{0}: (4, {}), {1}: (5, {})} | custom-call | flops 3623878656 | bytes 4718592 | tf_op jit(solution)/shard_map/mlp_part/pallas_call | solution.py:194
  242.9 9.2 %mlp_part.7 = (f32[512,768]{1,0:T(8,128)}, f32[512,768]{1,0:T(8,128)}, bf16[768,768]{1,0:T(8,128)(2,1)}, bf16[768,768]{1,0:T(8,128)(2,1)}) custom-call(bf16[512,768]{1,0:T(8,128)(2,1)} %multiply_convert_fusion.nm, bf16[512,768]{1,0:T(8,128)(2,1)} %bitcast.37.cot, bf16[768,768]{1,0:T(8,128)(2,1)} %bitcast.44.wu, ...), custom_call_target="tpu_custom_call", output_to_operand_aliasing={{0}: (4, {}), {1}: (5, {})} | custom-call | flops 3623878656 | bytes 4718592 | tf_op jit(solution)/shard_map/mlp_part/pallas_call | solution.py:194
  252.1 2.2 multiply_reduce_fusion
  254.3 1.8 multiply_add_fusion
  259.3 3.1 convolution_convert_fusion.1
  262.4 4.5 all-to-all-start.4
  274.4 4.7 all-to-all-done.4.datt
  279.2 3.5 all-to-all-start.3
  282.8 33.2 %attend_back.1 = bf16[4,576,512]{2,1,0:T(8,128)(2,1)} custom-call(s32[2]{0:T(128)} %pad_add_fusion.2.info, bf16[4,576,512]{2,1,0:T(8,128)(2,1)} %pad_maximum_fusion.qkv, bf16[4,192,512]{2,1,0:T(8,128)(2,1)} %get-tuple-element.27.att, bf16[4,192,512]{2,1,0:T(8,128)(2,1)} %all-to-all-done.4.datt, f32[3,4,1,512]{3,2,1,0:T(1,128)} %get-tuple-element.36.lse), custom_call_target="tpu_custom_call" | custom-call | flops 16106127360 | bytes 9437184 | tf_op jit(solution)/shard_map/attend_back/pallas_call | solution.py:137
  315.9 1.8 fusion.51
  321.6 4.0 collective-permute-start.35
  327.0 2.0 convolution_convert_fusion.4
  329.0 9.8 %collective-permute-done.42 = bf16[2,2,24,768]{3,2,1,0:T(8,128)(2,1)S(1)} collective-permute-done((bf16[2,2,24,768]{3,2,1,0:T(8,128)(2,1)S(1)}, bf16[2,2,24,768]{3,2,1,0:T(8,128)(2,1)S(1)}, u32[]{:S(2)}, u32[]{:S(2)}) %collective-permute-start.42) | collective-permute-done | bytes 147488 | tf_op jit(solution)/shard_map/ppermute | solution.py:213
  338.9 1.8 collective-permute-start.43
  341.5 1.8 collective-permute-done.43
  343.4 2.5 collective-permute-start.44
  346.0 2.3 collective-permute-done.44
  349.2 3.2 collective-permute-done.45
  352.9 1.7 add_convert_fusion
  354.6 1.8 collective-permute-start.36
  356.5 2.6 add_convert_fusion.3
  362.7 2.9 collective-permute-start.37
  365.6 5.6 %collective-permute-done.37 = bf16[96,576]{1,0:T(8,128)(2,1)S(1)} collective-permute-done((bf16[96,576]{1,0:T(8,128)(2,1)S(1)}, bf16[96,576]{1,0:T(8,128)(2,1)S(1)}, u32[]{:S(2)}, u32[]{:S(2)}) %collective-permute-start.37) | collective-permute-done | bytes 110624 | tf_op jit(solution)/shard_map/ppermute | solution.py:213
  372.5 7.9 %collective-permute-done.26 = bf16[512,768]{1,0:T(8,128)(2,1)S(1)} collective-permute-done((bf16[512,768]{1,0:T(8,128)(2,1)S(1)}, bf16[512,768]{1,0:T(8,128)(2,1)S(1)}, u32[]{:S(2)}, u32[]{:S(2)}) %collective-permute-start.26) | collective-permute-done | bytes 786464 | tf_op jit(solution)/shard_map/ppermute | solution.py:213
  385.7 21.4 %collective-permute-done.38 = bf16[96,576]{1,0:T(8,128)(2,1)S(1)} collective-permute-done((bf16[96,576]{1,0:T(8,128)(2,1)S(1)}, bf16[96,576]{1,0:T(8,128)(2,1)S(1)}, u32[]{:S(2)}, u32[]{:S(2)}) %collective-permute-start.38) | collective-permute-done | bytes 110624 | tf_op jit(solution)/shard_map/ppermute | solution.py:213
  410.5 1.7 collective-permute-done.31
  415.7 9.4 %collective-permute-done.32 = f32[8,768]{1,0:T(8,128)S(1)} collective-permute-done((f32[8,768]{1,0:T(8,128)S(1)}, f32[8,768]{1,0:T(8,128)S(1)}, u32[]{:S(2)}, u32[]{:S(2)}) %collective-permute-start.32) | collective-permute-done | bytes 24608 | tf_op jit(solution)/shard_map/ppermute | solution.py:213
  429.2 2.6 collective-permute-start.34
  431.8 2.2 fusion.39
  435.2 4.0 all-to-all-start.5
  439.3 2.7 add_convert_fusion.1
  442.1 2.1 collective-permute-start.56
  445.6 2.0 collective-permute-done.59
  447.6 15.3 %collective-permute-done.56 = bf16[2,2,96,768]{3,2,0,1:T(8,128)(2,1)S(1)} collective-permute-done((bf16[2,2,96,768]{3,2,0,1:T(8,128)(2,1)S(1)}, bf16[2,2,96,768]{3,2,0,1:T(8,128)(2,1)S(1)}, u32[]{:S(2)}, u32[]{:S(2)}) %collective-permute-start.56) | collective-permute-done | bytes 589856 | tf_op jit(solution)/shard_map/ppermute | solution.py:213
  465.9 8.6 %collective-permute-done.50 = bf16[2,2,96,768]{3,2,0,1:T(8,128)(2,1)S(1)} collective-permute-done((bf16[2,2,96,768]{3,2,0,1:T(8,128)(2,1)S(1)}, bf16[2,2,96,768]{3,2,0,1:T(8,128)(2,1)S(1)}, u32[]{:S(2)}, u32[]{:S(2)}) %collective-permute-start.50) | collective-permute-done | bytes 589856 | tf_op jit(solution)/shard_map/ppermute | solution.py:213
  476.3 2.6 collective-permute-start.61
  479.0 6.9 %collective-permute-done.51 = bf16[2,96,768]{2,1,0:T(8,128)(2,1)S(1)} collective-permute-done((bf16[2,96,768]{2,1,0:T(8,128)(2,1)S(1)}, bf16[2,96,768]{2,1,0:T(8,128)(2,1)S(1)}, u32[]{:S(2)}, u32[]{:S(2)}) %collective-permute-start.51) | collective-permute-done | bytes 294944 | tf_op jit(solution)/shard_map/ppermute | solution.py:213
  488.5 5.6 %collective-permute-done.52 = bf16[96,768]{1,0:T(8,128)(2,1)S(1)} collective-permute-done((bf16[96,768]{1,0:T(8,128)(2,1)S(1)}, bf16[96,768]{1,0:T(8,128)(2,1)S(1)}, u32[]{:S(2)}, u32[]{:S(2)}) %collective-permute-start.52) | collective-permute-done | bytes 147488 | tf_op jit(solution)/shard_map/ppermute | solution.py:213
  495.1 4.2 collective-permute-done.53
  502.9 2.2 copy.174
  505.1 3.6 reshape.322
  (390 shorter events, 114.8 us)
Async XLA Ops:
  1.7 46.9 %collective-permute-start.14 = (bf16[96,768]{1,0:T(8,128)(2,1)S(1)}, bf16[96,768]{1,0:T(8,128)(2,1)S(1)}, u32[]{:S(2)}, u32[]{:S(2)}) collective-permute-start(bf16[96,768]{1,0:T(8,128)(2,1)S(1)} %dynamic-slice_bitcast_fusion.9), channel_id=1, source_target_pairs={{0,4},{1,5},{2,6},{3,7},{4,0},{5,1},{6,2},{7,3},{8,12},{9,13},{10,... | collective-permute-start | bytes 442376 | tf_op jit(solution)/shard_map/ppermute | solution.py:213
  9.5 42.4 %collective-permute-start.11 = (bf16[96,768]{1,0:T(8,128)(2,1)S(1)}, bf16[96,768]{1,0:T(8,128)(2,1)S(1)}, u32[]{:S(2)}, u32[]{:S(2)}) collective-permute-start(bf16[96,768]{1,0:T(8,128)(2,1)S(1)} %reshape.288), channel_id=1, source_target_pairs={{0,4},{1,5},{2,6},{3,7},{4,0},{5,1},{6,2},{7,3},{8,12},{9,13},{10,... | collective-permute-start | bytes 442376 | tf_op jit(solution)/shard_map/ppermute | solution.py:213
  10.4 31.3 %collective-permute-start.6 = (bf16[24,768]{1,0:T(8,128)(2,1)S(1)}, bf16[24,768]{1,0:T(8,128)(2,1)S(1)}, u32[]{:S(2)}, u32[]{:S(2)}) collective-permute-start(bf16[24,768]{1,0:T(8,128)(2,1)S(1)} %dynamic-slice_bitcast_fusion.13), channel_id=1, source_target_pairs={{0,4},{1,5},{2,6},{3,7},{4,0},{5,1},{6,2},{7,3},{8,12},{9,13},{10,... | collective-permute-start | bytes 110600 | tf_op jit(solution)/shard_map/ppermute | solution.py:213
  14.7 33.3 %collective-permute-start = (bf16[96,640]{0,1:T(8,128)(2,1)S(1)}, bf16[96,640]{0,1:T(8,128)(2,1)S(1)}, u32[]{:S(2)}, u32[]{:S(2)}) collective-permute-start(bf16[96,640]{0,1:T(8,128)(2,1)S(1)} %maximum_maximum_fusion), channel_id=1, source_target_pairs={{0,4},{1,5},{2,6},{3,7},{4,0},{5,1},{6,2},{7,3},{8,12},{9,13},{10,... | collective-permute-start | bytes 368648 | tf_op jit(solution)/shard_map/ppermute | solution.py:213
  14.8 15.5 %collective-permute-start.27 = (s32[64,8]{0,1:T(8,128)S(1)}, s32[64,8]{0,1:T(8,128)S(1)}, u32[]{:S(2)}, u32[]{:S(2)}) collective-permute-start(s32[64,8]{0,1:T(8,128)S(1)} %copy-done.42), channel_id=1, source_target_pairs={{0,4},{1,5},{2,6},{3,7},{4,0},{5,1},{6,2},{7,3},{8,12},{9,13},{10,... | collective-permute-start | bytes 6152 | tf_op jit(solution)/shard_map/ppermute | solution.py:213
  19.2 82.9 %all-to-all-start = ((bf16[8,64,768]{2,1,0:T(8,128)(2,1)}), bf16[8,64,768]{2,1,0:T(8,128)(2,1)S(1)}, u32[]{:S(2)}, u32[]{:S(2)}) async-start(bf16[8,64,768]{2,1,0:T(8,128)(2,1)} %copy.147), calls=%async_computation | async-start | bytes 1572864 | tf_op jit(solution)/shard_map/all_to_all | solution.py:299
  30.3 9.8 %collective-permute-start.28 = (s32[2,64,8]{1,2,0:T(8,128)S(1)}, s32[2,64,8]{1,2,0:T(8,128)S(1)}, u32[]{:S(2)}, u32[]{:S(2)}) collective-permute-start(s32[2,64,8]{1,2,0:T(8,128)S(1)} %pad_add_fusion.1), channel_id=1, source_target_pairs={{0,2},{1,3},{2,0},{3,1},{4,6},{5,7},{6,4},{7,5},{8,10},{9,11},{10,... | collective-permute-start | bytes 12296 | tf_op jit(solution)/shard_map/ppermute | solution.py:213
  42.5 4.4 collective-permute-start.7
  46.9 6.1 %collective-permute-start.8 = (bf16[2,2,24,768]{3,2,1,0:T(8,128)(2,1)S(1)}, bf16[2,2,24,768]{3,2,1,0:T(8,128)(2,1)S(1)}, u32[]{:S(2)}, u32[]{:S(2)}) collective-permute-start(bf16[2,2,24,768]{3,2,1,0:T(8,128)(2,1)S(1)} %pad_maximum_fusion.17), channel_id=1, source_target_pairs={{0,1},{1,0},{2,3},{3,2},{4,5},{5,4},{6,7},{7,6},{8,9},{9,8},{10,11... | collective-permute-start | bytes 442376 | tf_op jit(solution)/shard_map/ppermute | solution.py:213
  48.2 10.6 %collective-permute-start.1 = (bf16[2,96,640]{1,2,0:T(8,128)(2,1)S(1)}, bf16[2,96,640]{1,2,0:T(8,128)(2,1)S(1)}, u32[]{:S(2)}, u32[]{:S(2)}) collective-permute-start(bf16[2,96,640]{1,2,0:T(8,128)(2,1)S(1)} %pad_maximum_fusion.10), channel_id=1, source_target_pairs={{0,2},{1,3},{2,0},{3,1},{4,6},{5,7},{6,4},{7,5},{8,10},{9,11},{10,... | collective-permute-start | bytes 737288 | tf_op jit(solution)/shard_map/ppermute | solution.py:213
  50.3 15.0 %collective-permute-start.15 = (bf16[2,96,768]{2,1,0:T(8,128)(2,1)}, bf16[2,96,768]{2,1,0:T(8,128)(2,1)}, u32[]{:S(2)}, u32[]{:S(2)}) collective-permute-start(bf16[2,96,768]{2,1,0:T(8,128)(2,1)} %pad_maximum_fusion.13), channel_id=1, source_target_pairs={{0,2},{1,3},{2,0},{3,1},{4,6},{5,7},{6,4},{7,5},{8,10},{9,11},{10,... | collective-permute-start | bytes 884744 | tf_op jit(solution)/shard_map/ppermute | solution.py:213
  52.7 17.3 %collective-permute-start.12 = (bf16[2,96,768]{2,1,0:T(8,128)(2,1)}, bf16[2,96,768]{2,1,0:T(8,128)(2,1)}, u32[]{:S(2)}, u32[]{:S(2)}) collective-permute-start(bf16[2,96,768]{2,1,0:T(8,128)(2,1)} %pad_maximum_fusion.12), channel_id=1, source_target_pairs={{0,2},{1,3},{2,0},{3,1},{4,6},{5,7},{6,4},{7,5},{8,10},{9,11},{10,... | collective-permute-start | bytes 884744 | tf_op jit(solution)/shard_map/ppermute | solution.py:213
  53.9 18.7 %collective-permute-start.9 = (bf16[2,2,2,24,768]{4,3,2,1,0:T(8,128)(2,1)}, bf16[2,2,2,24,768]{4,3,2,1,0:T(8,128)(2,1)}, u32[]{:S(2)}, u32[]{:S(2)}) collective-permute-start(bf16[2,2,2,24,768]{4,3,2,1,0:T(8,128)(2,1)} %pad_maximum_fusion.11), channel_id=1, source_target_pairs={{0,16},{8,24},{16,0},{24,8},{1,17},{9,25},{17,1},{25,9},{2,18},{10... | collective-permute-start | bytes 884744 | tf_op jit(solution)/shard_map/ppermute | solution.py:213
  60.1 14.5 %collective-permute-start.2 = (bf16[2,2,96,640]{3,2,1,0:T(8,128)(2,1)}, bf16[2,2,96,640]{3,2,1,0:T(8,128)(2,1)}, u32[]{:S(2)}, u32[]{:S(2)}) collective-permute-start(bf16[2,2,96,640]{3,2,1,0:T(8,128)(2,1)} %copy.149), channel_id=1, source_target_pairs={{0,1},{1,0},{2,3},{3,2},{4,5},{5,4},{6,7},{7,6},{8,9},{9,8},{10,11... | collective-permute-start | bytes 1474568 | tf_op jit(solution)/shard_map/ppermute | solution.py:213
  67.2 76.4 %collective-permute-start.20 = (bf16[2,2,96,768]{3,2,0,1:T(8,128)(2,1)}, bf16[2,2,96,768]{3,2,0,1:T(8,128)(2,1)}, u32[]{:S(2)}, u32[]{:S(2)}) collective-permute-start(bf16[2,2,96,768]{3,2,0,1:T(8,128)(2,1)} %pad_maximum_fusion.9), channel_id=1, source_target_pairs={{0,16},{8,24},{16,0},{24,8},{1,17},{9,25},{17,1},{25,9},{2,18},{10... | collective-permute-start | bytes 1769480 | tf_op jit(solution)/shard_map/ppermute | solution.py:213
  68.7 31.1 %collective-permute-start.16 = (bf16[2,2,96,768]{3,2,0,1:T(8,128)(2,1)}, bf16[2,2,96,768]{3,2,0,1:T(8,128)(2,1)}, u32[]{:S(2)}, u32[]{:S(2)}) collective-permute-start(bf16[2,2,96,768]{3,2,0,1:T(8,128)(2,1)} %pad_maximum_fusion.9), channel_id=1, source_target_pairs={{0,1},{1,0},{2,3},{3,2},{4,5},{5,4},{6,7},{7,6},{8,9},{9,8},{10,11... | collective-permute-start | bytes 1769480 | tf_op jit(solution)/shard_map/ppermute | solution.py:213
  71.9 23.9 %collective-permute-start.13 = (bf16[2,2,96,768]{3,2,0,1:T(8,128)(2,1)}, bf16[2,2,96,768]{3,2,0,1:T(8,128)(2,1)}, u32[]{:S(2)}, u32[]{:S(2)}) collective-permute-start(bf16[2,2,96,768]{3,2,0,1:T(8,128)(2,1)} %pad_maximum_fusion.8), channel_id=1, source_target_pairs={{0,1},{1,0},{2,3},{3,2},{4,5},{5,4},{6,7},{7,6},{8,9},{9,8},{10,11... | collective-permute-start | bytes 1769480 | tf_op jit(solution)/shard_map/ppermute | solution.py:213
  74.6 99.3 %collective-permute-start.10 = (bf16[2,2,2,2,24,768]{5,4,3,2,1,0:T(8,128)(2,1)}, bf16[2,2,2,2,24,768]{5,4,3,2,1,0:T(8,128)(2,1)}, u32[]{:S(2)}, u32[]{:S(2)}) collective-permute-start(bf16[2,2,2,2,24,768]{5,4,3,2,1,0:T(8,128)(2,1)} %pad_maximum_fusion.7), channel_id=1, source_target_pairs={{0,8},{8,0},{16,24},{24,16},{1,9},{9,1},{17,25},{25,17},{2,10},{10... | collective-permute-start | bytes 1769480 | tf_op jit(solution)/shard_map/ppermute | solution.py:213
  98.2 96.8 %collective-permute-start.19 = (bf16[768,768]{1,0:T(8,128)(2,1)}, bf16[768,768]{1,0:T(8,128)(2,1)}, u32[]{:S(2)}, u32[]{:S(2)}) collective-permute-start(bf16[768,768]{1,0:T(8,128)(2,1)} %bitcast.44.wu), channel_id=1, source_target_pairs={{0,16},{8,24},{16,0},{24,8},{1,17},{9,25},{17,1},{25,9},{2,18},{10... | collective-permute-start | bytes 3538952 | tf_op jit(solution)/shard_map/ppermute | solution.py:213
  102.1 38.9 %collective-permute-start.4 = (bf16[512,768]{1,0:T(8,128)(2,1)S(1)}, bf16[512,768]{1,0:T(8,128)(2,1)S(1)}, u32[]{:S(2)}, u32[]{:S(2)}) collective-permute-start(bf16[512,768]{1,0:T(8,128)(2,1)S(1)} %bitcast.292), channel_id=1, source_target_pairs={{0,16},{8,24},{16,0},{24,8},{1,17},{9,25},{17,1},{25,9},{2,18},{10... | collective-permute-start | bytes 2359304 | tf_op jit(solution)/shard_map/ppermute | solution.py:213
  105.5 128.0 %collective-permute-start.17 = (bf16[768,768]{1,0:T(8,128)(2,1)}, bf16[768,768]{1,0:T(8,128)(2,1)}, u32[]{:S(2)}, u32[]{:S(2)}) collective-permute-start(bf16[768,768]{1,0:T(8,128)(2,1)} %bitcast.44.wu), channel_id=1, source_target_pairs={{0,8},{8,0},{16,24},{24,16},{1,9},{9,1},{17,25},{25,17},{2,10},{10... | collective-permute-start | bytes 3538952 | tf_op jit(solution)/shard_map/ppermute | solution.py:213
  143.6 89.9 %collective-permute-start.18 = (bf16[768,768]{1,0:T(8,128)(2,1)}, bf16[768,768]{1,0:T(8,128)(2,1)}, u32[]{:S(2)}, u32[]{:S(2)}) collective-permute-start(bf16[768,768]{1,0:T(8,128)(2,1)} %bitcast.53.wd), channel_id=1, source_target_pairs={{0,8},{8,0},{16,24},{24,16},{1,9},{9,1},{17,25},{25,17},{2,10},{10... | collective-permute-start | bytes 3538952 | tf_op jit(solution)/shard_map/ppermute | solution.py:213
  144.2 31.9 %collective-permute-start.21 = (bf16[2,2,96,768]{3,2,0,1:T(8,128)(2,1)}, bf16[2,2,96,768]{3,2,0,1:T(8,128)(2,1)}, u32[]{:S(2)}, u32[]{:S(2)}) collective-permute-start(bf16[2,2,96,768]{3,2,0,1:T(8,128)(2,1)} %collective-permute-done.20), channel_id=1, source_target_pairs={{0,1},{1,0},{2,3},{3,2},{4,5},{5,4},{6,7},{7,6},{8,9},{9,8},{10,11... | collective-permute-start | bytes 1769480 | tf_op jit(solution)/shard_map/ppermute | solution.py:213
  169.8 15.6 %all-to-all-start.1 = ((bf16[4,192,512]{2,1,0:T(8,128)(2,1)}), bf16[4,192,512]{2,1,0:T(8,128)(2,1)S(1)}, u32[]{:S(2)}, u32[]{:S(2)}) async-start(bf16[4,192,512]{2,1,0:T(8,128)(2,1)} %get-tuple-element.27.att), calls=%async_computation.1 | async-start | bytes 1572864 | tf_op jit(solution)/shard_map/all_to_all | solution.py:333
  185.4 28.4 %all-to-all-start.2 = ((bf16[8,64,768]{2,1,0:T(8,128)(2,1)}), bf16[8,64,768]{2,1,0:T(8,128)(2,1)}, u32[]{:S(2)}, u32[]{:S(2)}) async-start(bf16[8,64,768]{2,1,0:T(8,128)(2,1)} %bitcast.286), calls=%async_computation.2 | async-start | bytes 1572864 | tf_op jit(solution)/shard_map/all_to_all | solution.py:299
  195.1 18.8 %collective-permute-start.23 = (bf16[768,768]{1,0:T(8,128)(2,1)}, bf16[768,768]{1,0:T(8,128)(2,1)}, u32[]{:S(2)}, u32[]{:S(2)}) collective-permute-start(bf16[768,768]{1,0:T(8,128)(2,1)} %bitcast.56.wd), channel_id=1, source_target_pairs={{0,8},{8,0},{16,24},{24,16},{1,9},{9,1},{17,25},{25,17},{2,10},{10... | collective-permute-start | bytes 3538952 | tf_op jit(solution)/shard_map/ppermute | solution.py:213
  195.1 18.8 %collective-permute-start.22 = (bf16[768,768]{1,0:T(8,128)(2,1)}, bf16[768,768]{1,0:T(8,128)(2,1)}, u32[]{:S(2)}, u32[]{:S(2)}) collective-permute-start(bf16[768,768]{1,0:T(8,128)(2,1)} %collective-permute-done.19.wu), channel_id=1, source_target_pairs={{0,8},{8,0},{16,24},{24,16},{1,9},{9,1},{17,25},{25,17},{2,10},{10... | collective-permute-start | bytes 3538952 | tf_op jit(solution)/shard_map/ppermute | solution.py:213
  259.2 10.9 %collective-permute-start.40 = (bf16[2,2,2,2,24,768]{5,4,3,2,1,0:T(8,128)(2,1)}, bf16[2,2,2,2,24,768]{5,4,3,2,1,0:T(8,128)(2,1)}, u32[]{:S(2)}, u32[]{:S(2)}) collective-permute-start(bf16[2,2,2,2,24,768]{5,4,3,2,1,0:T(8,128)(2,1)} %dynamic-slice_bitcast_fusion), channel_id=1, source_target_pairs={{0,8},{8,0},{16,24},{24,16},{1,9},{9,1},{17,25},{25,17},{2,10},{10... | collective-permute-start | bytes 1769480 | tf_op jit(solution)/shard_map/ppermute | solution.py:213
  262.4 16.8 %all-to-all-start.4 = ((bf16[4,192,512]{2,1,0:T(8,128)(2,1)}), bf16[4,192,512]{2,1,0:T(8,128)(2,1)}, u32[]{:S(2)}, u32[]{:S(2)}) async-start(bf16[4,192,512]{2,1,0:T(8,128)(2,1)} %bitcast.323), calls=%async_computation.4 | async-start | bytes 1572864 | tf_op jit(solution)/shard_map/all_to_all | solution.py:333
  268.1 84.3 %collective-permute-start.57 = (bf16[768,768]{1,0:T(8,128)(2,1)}, bf16[768,768]{1,0:T(8,128)(2,1)}, u32[]{:S(2)}, u32[]{:S(2)}) collective-permute-start(bf16[768,768]{1,0:T(8,128)(2,1)} %get-tuple-element.44), channel_id=1, source_target_pairs={{0,8},{8,0},{16,24},{24,16},{1,9},{9,1},{17,25},{25,17},{2,10},{10... | collective-permute-start | bytes 3538952 | tf_op jit(solution)/shard_map/ppermute | solution.py:213
  268.6 86.0 %collective-permute-start.48 = (bf16[768,768]{1,0:T(8,128)(2,1)}, bf16[768,768]{1,0:T(8,128)(2,1)}, u32[]{:S(2)}, u32[]{:S(2)}) collective-permute-start(bf16[768,768]{1,0:T(8,128)(2,1)} %get-tuple-element.40), channel_id=1, source_target_pairs={{0,8},{8,0},{16,24},{24,16},{1,9},{9,1},{17,25},{25,17},{2,10},{10... | collective-permute-start | bytes 3538952 | tf_op jit(solution)/shard_map/ppermute | solution.py:213
  268.6 170.6 %collective-permute-start.47 = (bf16[768,768]{1,0:T(8,128)(2,1)}, bf16[768,768]{1,0:T(8,128)(2,1)}, u32[]{:S(2)}, u32[]{:S(2)}) collective-permute-start(bf16[768,768]{1,0:T(8,128)(2,1)} %get-tuple-element.38), channel_id=1, source_target_pairs={{0,8},{8,0},{16,24},{24,16},{1,9},{9,1},{17,25},{25,17},{2,10},{10... | collective-permute-start | bytes 3538952 | tf_op jit(solution)/shard_map/ppermute | solution.py:213
  272.8 52.8 %collective-permute-start.41 = (bf16[2,2,2,24,768]{4,3,2,1,0:T(8,128)(2,1)}, bf16[2,2,2,24,768]{4,3,2,1,0:T(8,128)(2,1)}, u32[]{:S(2)}, u32[]{:S(2)}) collective-permute-start(bf16[2,2,2,24,768]{4,3,2,1,0:T(8,128)(2,1)} %dynamic-slice_bitcast_fusion.4), channel_id=1, source_target_pairs={{0,16},{8,24},{16,0},{24,8},{1,17},{9,25},{17,1},{25,9},{2,18},{10... | collective-permute-start | bytes 884744 | tf_op jit(solution)/shard_map/ppermute | solution.py:213
  279.2 133.8 %all-to-all-start.3 = ((bf16[8,64,768]{2,1,0:T(8,128)(2,1)}), bf16[8,64,768]{2,1,0:T(8,128)(2,1)S(1)}, u32[]{:S(2)}, u32[]{:S(2)}) async-start(bf16[8,64,768]{2,1,0:T(8,128)(2,1)} %bitcast.57), calls=%async_computation.3 | async-start | bytes 1572864 | tf_op jit(solution)/shard_map/all_to_all | solution.py:299
  321.6 21.7 %collective-permute-start.35 = (bf16[2,2,96,576]{3,2,1,0:T(8,128)(2,1)S(1)}, bf16[2,2,96,576]{3,2,1,0:T(8,128)(2,1)S(1)}, u32[]{:S(2)}, u32[]{:S(2)}) collective-permute-start(bf16[2,2,96,576]{3,2,1,0:T(8,128)(2,1)S(1)} %dynamic-slice_bitcast_fusion.1), channel_id=1, source_target_pairs={{0,1},{1,0},{2,3},{3,2},{4,5},{5,4},{6,7},{7,6},{8,9},{9,8},{10,11... | collective-permute-start | bytes 1327112 | tf_op jit(solution)/shard_map/ppermute | solution.py:213
  326.8 12.0 %collective-permute-start.42 = (bf16[2,2,24,768]{3,2,1,0:T(8,128)(2,1)S(1)}, bf16[2,2,24,768]{3,2,1,0:T(8,128)(2,1)S(1)}, u32[]{:S(2)}, u32[]{:S(2)}) collective-permute-start(bf16[2,2,24,768]{3,2,1,0:T(8,128)(2,1)S(1)} %dynamic-slice_bitcast_fusion.8), channel_id=1, source_target_pairs={{0,1},{1,0},{2,3},{3,2},{4,5},{5,4},{6,7},{7,6},{8,9},{9,8},{10,11... | collective-permute-start | bytes 442376 | tf_op jit(solution)/shard_map/ppermute | solution.py:213
  338.9 4.4 collective-permute-start.43
  343.3 95.9 %collective-permute-start.55 = (bf16[768,768]{1,0:T(8,128)(2,1)}, bf16[768,768]{1,0:T(8,128)(2,1)}, u32[]{:S(2)}, u32[]{:S(2)}) collective-permute-start(bf16[768,768]{1,0:T(8,128)(2,1)} %get-tuple-element.42), channel_id=1, source_target_pairs={{0,8},{8,0},{16,24},{24,16},{1,9},{9,1},{17,25},{25,17},{2,10},{10... | collective-permute-start | bytes 3538952 | tf_op jit(solution)/shard_map/ppermute | solution.py:213
  343.4 4.9 collective-permute-start.44
  348.3 4.0 collective-permute-start.45
  352.3 6.8 %collective-permute-start.25 = (bf16[512,768]{1,0:T(8,128)(2,1)S(1)}, bf16[512,768]{1,0:T(8,128)(2,1)S(1)}, u32[]{:S(2)}, u32[]{:S(2)}) collective-permute-start(bf16[512,768]{1,0:T(8,128)(2,1)S(1)} %convolution_convert_fusion.2), channel_id=1, source_target_pairs={{0,8},{8,0},{16,24},{24,16},{1,9},{9,1},{17,25},{25,17},{2,10},{10... | collective-permute-start | bytes 2359304 | tf_op jit(solution)/shard_map/ppermute | solution.py:213
  352.4 20.1 %collective-permute-start.24 = (bf16[512,768]{1,0:T(8,128)(2,1)S(1)}, bf16[512,768]{1,0:T(8,128)(2,1)S(1)}, u32[]{:S(2)}, u32[]{:S(2)}) collective-permute-start(bf16[512,768]{1,0:T(8,128)(2,1)S(1)} %convolution_convert_fusion.4), channel_id=1, source_target_pairs={{0,8},{8,0},{16,24},{24,16},{1,9},{9,1},{17,25},{25,17},{2,10},{10... | collective-permute-start | bytes 2359304 | tf_op jit(solution)/shard_map/ppermute | solution.py:213
  354.6 8.0 %collective-permute-start.36 = (bf16[2,96,576]{2,1,0:T(8,128)(2,1)S(1)}, bf16[2,96,576]{2,1,0:T(8,128)(2,1)S(1)}, u32[]{:S(2)}, u32[]{:S(2)}) collective-permute-start(bf16[2,96,576]{2,1,0:T(8,128)(2,1)S(1)} %dynamic-slice_bitcast_fusion.5), channel_id=1, source_target_pairs={{0,2},{1,3},{2,0},{3,1},{4,6},{5,7},{6,4},{7,5},{8,10},{9,11},{10,... | collective-permute-start | bytes 663560 | tf_op jit(solution)/shard_map/ppermute | solution.py:213
  359.9 20.5 %collective-permute-start.26 = (bf16[512,768]{1,0:T(8,128)(2,1)S(1)}, bf16[512,768]{1,0:T(8,128)(2,1)S(1)}, u32[]{:S(2)}, u32[]{:S(2)}) collective-permute-start(bf16[512,768]{1,0:T(8,128)(2,1)S(1)} %add_convert_fusion.6), channel_id=1, source_target_pairs={{0,16},{8,24},{16,0},{24,8},{1,17},{9,25},{17,1},{25,9},{2,18},{10... | collective-permute-start | bytes 2359304 | tf_op jit(solution)/shard_map/ppermute | solution.py:213
  362.7 8.5 %collective-permute-start.37 = (bf16[96,576]{1,0:T(8,128)(2,1)S(1)}, bf16[96,576]{1,0:T(8,128)(2,1)S(1)}, u32[]{:S(2)}, u32[]{:S(2)}) collective-permute-start(bf16[96,576]{1,0:T(8,128)(2,1)S(1)} %dynamic-slice_bitcast_fusion.10), channel_id=1, source_target_pairs={{0,4},{1,5},{2,6},{3,7},{4,0},{5,1},{6,2},{7,3},{8,12},{9,13},{10,... | collective-permute-start | bytes 331784 | tf_op jit(solution)/shard_map/ppermute | solution.py:213
  371.2 68.1 %collective-permute-start.49 = (bf16[768,768]{1,0:T(8,128)(2,1)}, bf16[768,768]{1,0:T(8,128)(2,1)}, u32[]{:S(2)}, u32[]{:S(2)}) collective-permute-start(bf16[768,768]{1,0:T(8,128)(2,1)} %add_convert_fusion.3), channel_id=1, source_target_pairs={{0,16},{8,24},{16,0},{24,8},{1,17},{9,25},{17,1},{25,9},{2,18},{10... | collective-permute-start | bytes 3538952 | tf_op jit(solution)/shard_map/ppermute | solution.py:213
  372.4 36.8 %collective-permute-start.46 = (bf16[2,24,768]{2,1,0:T(8,128)(2,1)S(1)}, bf16[2,24,768]{2,1,0:T(8,128)(2,1)S(1)}, u32[]{:S(2)}, u32[]{:S(2)}) collective-permute-start(bf16[2,24,768]{2,1,0:T(8,128)(2,1)S(1)} %pad_maximum_fusion.19), channel_id=1, source_target_pairs={{0,8},{8,0},{16,24},{24,16},{1,9},{9,1},{17,25},{25,17},{2,10},{10... | collective-permute-start | bytes 221192 | tf_op jit(solution)/shard_map/ppermute | solution.py:213
  380.4 26.7 %collective-permute-start.38 = (bf16[96,576]{1,0:T(8,128)(2,1)S(1)}, bf16[96,576]{1,0:T(8,128)(2,1)S(1)}, u32[]{:S(2)}, u32[]{:S(2)}) collective-permute-start(bf16[96,576]{1,0:T(8,128)(2,1)S(1)} %fusion.60), channel_id=1, source_target_pairs={{0,16},{8,24},{16,0},{24,8},{1,17},{9,25},{17,1},{25,9},{2,18},{10... | collective-permute-start | bytes 331784 | tf_op jit(solution)/shard_map/ppermute | solution.py:213
  408.4 3.8 collective-permute-start.31
  409.2 22.6 %collective-permute-start.58 = (bf16[2,2,96,768]{3,2,0,1:T(8,128)(2,1)}, bf16[2,2,96,768]{3,2,0,1:T(8,128)(2,1)}, u32[]{:S(2)}, u32[]{:S(2)}) collective-permute-start(bf16[2,2,96,768]{3,2,0,1:T(8,128)(2,1)} %bitcast.287), channel_id=1, source_target_pairs={{0,1},{1,0},{2,3},{3,2},{4,5},{5,4},{6,7},{7,6},{8,9},{9,8},{10,11... | collective-permute-start | bytes 1769480 | tf_op jit(solution)/shard_map/ppermute | solution.py:213
  414.3 10.8 %collective-permute-start.32 = (f32[8,768]{1,0:T(8,128)S(1)}, f32[8,768]{1,0:T(8,128)S(1)}, u32[]{:S(2)}, u32[]{:S(2)}) collective-permute-start(f32[8,768]{1,0:T(8,128)S(1)} %add.253), channel_id=1, source_target_pairs={{0,1},{1,0},{2,3},{3,2},{4,5},{5,4},{6,7},{7,6},{8,9},{9,8},{10,11... | collective-permute-start | bytes 73736 | tf_op jit(solution)/shard_map/ppermute | solution.py:213
  425.1 4.1 collective-permute-start.33
  429.2 10.0 %collective-permute-start.34 = (f32[8,768]{1,0:T(8,128)S(1)}, f32[8,768]{1,0:T(8,128)S(1)}, u32[]{:S(2)}, u32[]{:S(2)}) collective-permute-start(f32[8,768]{1,0:T(8,128)S(1)} %add.255), channel_id=1, source_target_pairs={{0,4},{1,5},{2,6},{3,7},{4,0},{5,1},{6,2},{7,3},{8,12},{9,13},{10,... | collective-permute-start | bytes 73736 | tf_op jit(solution)/shard_map/ppermute | solution.py:213
  434.0 13.7 %collective-permute-start.59 = (bf16[2,2,96,768]{3,2,0,1:T(8,128)(2,1)}, bf16[2,2,96,768]{3,2,0,1:T(8,128)(2,1)}, u32[]{:S(2)}, u32[]{:S(2)}) collective-permute-start(bf16[2,2,96,768]{3,2,0,1:T(8,128)(2,1)} %fusion.39), channel_id=1, source_target_pairs={{0,16},{8,24},{16,0},{24,8},{1,17},{9,25},{17,1},{25,9},{2,18},{10... | collective-permute-start | bytes 1769480 | tf_op jit(solution)/shard_map/ppermute | solution.py:213
  435.2 64.3 %all-to-all-start.5 = ((bf16[8,64,768]{2,1,0:T(8,128)(2,1)}), bf16[8,64,768]{2,1,0:T(8,128)(2,1)S(1)}, u32[]{:S(2)}, u32[]{:S(2)}) async-start(bf16[8,64,768]{2,1,0:T(8,128)(2,1)} %bitcast.64), calls=%async_computation.5 | async-start | bytes 1572864 | tf_op jit(solution)/shard_map/all_to_all | solution.py:299
  442.1 20.9 %collective-permute-start.56 = (bf16[2,2,96,768]{3,2,0,1:T(8,128)(2,1)S(1)}, bf16[2,2,96,768]{3,2,0,1:T(8,128)(2,1)S(1)}, u32[]{:S(2)}, u32[]{:S(2)}) collective-permute-start(bf16[2,2,96,768]{3,2,0,1:T(8,128)(2,1)S(1)} %bitcast.324), channel_id=1, source_target_pairs={{0,1},{1,0},{2,3},{3,2},{4,5},{5,4},{6,7},{7,6},{8,9},{9,8},{10,11... | collective-permute-start | bytes 1769480 | tf_op jit(solution)/shard_map/ppermute | solution.py:213
  444.3 30.2 %collective-permute-start.50 = (bf16[2,2,96,768]{3,2,0,1:T(8,128)(2,1)S(1)}, bf16[2,2,96,768]{3,2,0,1:T(8,128)(2,1)S(1)}, u32[]{:S(2)}, u32[]{:S(2)}) collective-permute-start(bf16[2,2,96,768]{3,2,0,1:T(8,128)(2,1)S(1)} %bitcast.325), channel_id=1, source_target_pairs={{0,1},{1,0},{2,3},{3,2},{4,5},{5,4},{6,7},{7,6},{8,9},{9,8},{10,11... | collective-permute-start | bytes 1769480 | tf_op jit(solution)/shard_map/ppermute | solution.py:213
  464.3 11.9 %collective-permute-start.60 = (bf16[2,96,768]{2,1,0:T(8,128)(2,1)S(1)}, bf16[2,96,768]{2,1,0:T(8,128)(2,1)S(1)}, u32[]{:S(2)}, u32[]{:S(2)}) collective-permute-start(bf16[2,96,768]{2,1,0:T(8,128)(2,1)S(1)} %dynamic-slice_bitcast_fusion.2), channel_id=1, source_target_pairs={{0,2},{1,3},{2,0},{3,1},{4,6},{5,7},{6,4},{7,5},{8,10},{9,11},{10,... | collective-permute-start | bytes 884744 | tf_op jit(solution)/shard_map/ppermute | solution.py:213
  474.7 11.2 %collective-permute-start.51 = (bf16[2,96,768]{2,1,0:T(8,128)(2,1)S(1)}, bf16[2,96,768]{2,1,0:T(8,128)(2,1)S(1)}, u32[]{:S(2)}, u32[]{:S(2)}) collective-permute-start(bf16[2,96,768]{2,1,0:T(8,128)(2,1)S(1)} %dynamic-slice_bitcast_fusion.3), channel_id=1, source_target_pairs={{0,2},{1,3},{2,0},{3,1},{4,6},{5,7},{6,4},{7,5},{8,10},{9,11},{10,... | collective-permute-start | bytes 884744 | tf_op jit(solution)/shard_map/ppermute | solution.py:213
  476.3 11.3 %collective-permute-start.61 = (bf16[96,768]{1,0:T(8,128)(2,1)S(1)}, bf16[96,768]{1,0:T(8,128)(2,1)S(1)}, u32[]{:S(2)}, u32[]{:S(2)}) collective-permute-start(bf16[96,768]{1,0:T(8,128)(2,1)S(1)} %dynamic-slice_bitcast_fusion.6), channel_id=1, source_target_pairs={{0,4},{1,5},{2,6},{3,7},{4,0},{5,1},{6,2},{7,3},{8,12},{9,13},{10,... | collective-permute-start | bytes 442376 | tf_op jit(solution)/shard_map/ppermute | solution.py:213
  486.0 8.1 %collective-permute-start.52 = (bf16[96,768]{1,0:T(8,128)(2,1)S(1)}, bf16[96,768]{1,0:T(8,128)(2,1)S(1)}, u32[]{:S(2)}, u32[]{:S(2)}) collective-permute-start(bf16[96,768]{1,0:T(8,128)(2,1)S(1)} %dynamic-slice_bitcast_fusion.7), channel_id=1, source_target_pairs={{0,4},{1,5},{2,6},{3,7},{4,0},{5,1},{6,2},{7,3},{8,12},{9,13},{10,... | collective-permute-start | bytes 442376 | tf_op jit(solution)/shard_map/ppermute | solution.py:213
  487.7 7.3 %collective-permute-start.62 = (bf16[96,768]{1,0:T(8,128)(2,1)S(1)}, bf16[96,768]{1,0:T(8,128)(2,1)S(1)}, u32[]{:S(2)}, u32[]{:S(2)}) collective-permute-start(bf16[96,768]{1,0:T(8,128)(2,1)S(1)} %fusion.57), channel_id=1, source_target_pairs={{0,16},{8,24},{16,0},{24,8},{1,17},{9,25},{17,1},{25,9},{2,18},{10... | collective-permute-start | bytes 442376 | tf_op jit(solution)/shard_map/ppermute | solution.py:213
  494.1 5.2 %collective-permute-start.53 = (bf16[96,768]{1,0:T(8,128)(2,1)S(1)}, bf16[96,768]{1,0:T(8,128)(2,1)S(1)}, u32[]{:S(2)}, u32[]{:S(2)}) collective-permute-start(bf16[96,768]{1,0:T(8,128)(2,1)S(1)} %fusion.58), channel_id=1, source_target_pairs={{0,16},{8,24},{16,0},{24,8},{1,17},{9,25},{17,1},{25,9},{2,18},{10... | collective-permute-start | bytes 442376 | tf_op jit(solution)/shard_map/ppermute | solution.py:213
  495.0 5.8 %collective-permute-start.63 = (bf16[2,96,768]{2,1,0:T(8,128)(2,1)S(1)}, bf16[2,96,768]{2,1,0:T(8,128)(2,1)S(1)}, u32[]{:S(2)}, u32[]{:S(2)}) collective-permute-start(bf16[2,96,768]{2,1,0:T(8,128)(2,1)S(1)} %pad_maximum_fusion.15), channel_id=1, source_target_pairs={{0,8},{8,0},{16,24},{24,16},{1,9},{9,1},{17,25},{25,17},{2,10},{10... | collective-permute-start | bytes 884744 | tf_op jit(solution)/shard_map/ppermute | solution.py:213
  (67 other events, 547.9 us)
